TPU v7x, 32 devices: a whole 2x2x4 slice. The times are simulated.
32 devices in a mesh: member: 8 (over z, x), space: 4 (over y, core).
Axes of the slice: x: 2, y: 2, z: 4, core: 2. Of those that a mesh axis runs over, the one named last changes fastest.
Arguments:
- states: float32 [1024, 24576], P('member', 'space'), may hold values from -6 to 6
- obs_values: float32 [2, 2048], replicated, may hold values from -6 to 6
- obs_weights: float32 [2, 2048], replicated, may hold values from 0.2 to 2
- obs_cell: int32 [2, 4, 4], P(None, 'space'), may hold values from 0 to 47
- op_select: int32 [2, 4, 4], P(None, 'space'), may hold values from 0 to 7
- op_table: float32 [8, 128, 128], replicated, may hold values from -0.5 to 0.5
- loc_obs: int32 [2, 4, 48, 8], P(None, 'space', 'member'), may hold values from 0 to 11
- loc_tile: int32 [2, 4, 48, 8], P(None, 'space', 'member'), may hold values from 0 to 7
- loc_tiles: float32 [8, 128, 128], replicated, may hold values from 0 to 1
Outputs:
- analysis: float32 [1024, 24576], P('member', 'space')
All inputs are finite; a program needn't handle non-finite values.
Results may differ from a plain program's by a relative error of at most 0.00012.
Values sent between devices are 32-bit elements; how exact they have to be, the bound alone decides.
A program may use at most 128 MiB of HBM per device.

v0:
```python
import functools

import jax
import jax.numpy as jnp
from jax import lax
from jax.experimental import pallas as pl
from jax.experimental.pallas import tpu as pltpu
from jax.sharding import PartitionSpec as P

BLK = 128
NT_DIMS = (((1,), (1,)), ((), ()))


def split(x):
    hi = x.astype(jnp.bfloat16)
    lo = (x - hi.astype(jnp.float32)).astype(jnp.bfloat16)
    return hi, lo


def dot(a, b):
    return jnp.dot(a, b, preferred_element_type=jnp.float32)


def dot_nt(a, b):
    return lax.dot_general(a, b, NT_DIMS, preferred_element_type=jnp.float32)


def send(src, dst, send_sem, recv_sem, member, space):
    return pltpu.make_async_remote_copy(
        src_ref=src,
        dst_ref=dst,
        send_sem=send_sem,
        recv_sem=recv_sem,
        device_id=(member, space),
        device_id_type=pl.DeviceIdType.MESH,
    )


def columns(ref, block):
    return ref.at[:, pl.ds(pl.multiple_of(block * BLK, BLK), BLK)]


def ring_of_slabs(space_n):
    slab = lax.axis_index("space")
    return slab, lax.rem(slab + 1, space_n), lax.rem(slab + space_n - 1, space_n)


def load_window(batch_no, ob, space_n, window, values_ref, weights_ref, scratch):
    hi_ref, lo_ref, d_ref, w_ref = scratch[:4]
    members = window[0].shape[0]
    slab = lax.axis_index("space")
    for place, ref in enumerate(window):
        source = lax.rem(slab + space_n - 1 + place, space_n)
        for o in range(ob):
            j = place * ob + o
            row = (batch_no * space_n + source) * ob + o
            block = ref[:, o * BLK:(o + 1) * BLK]
            mean = jnp.sum(block, axis=0, keepdims=True) * (1.0 / members)
            hi, lo = split(block - mean)
            hi_ref[j] = hi
            lo_ref[j] = lo
            w_ref[j] = weights_ref[row]
            d_ref[j] = weights_ref[row] * (values_ref[row] - mean)


def update(cell, picks, tiles_ref, scratch):
    hi_ref, lo_ref, d_ref, w_ref, acc_ref = scratch
    members = cell.shape[0]
    mean = jnp.sum(cell, axis=0, keepdims=True) * (1.0 / members)
    hi, lo = split(jnp.transpose(cell - mean))
    both = jnp.concatenate([hi, lo], axis=0)
    ones = []
    for pair in range(len(picks) // 2):
        (first, tile_a), (second, tile_b) = picks[2 * pair], picks[2 * pair + 1]
        obs_hi = jnp.concatenate([hi_ref[first], hi_ref[second]], axis=1)
        obs_lo = jnp.concatenate([lo_ref[first], lo_ref[second]], axis=1)
        part = dot(both, obs_hi)
        cov = part[:BLK] + part[BLK:] + dot(hi, obs_lo)
        tile = jnp.concatenate([tiles_ref[tile_a], tiles_ref[tile_b]], axis=1)
        gain = tile * (cov * (1.0 / (members - 1)))
        d = jnp.concatenate([d_ref[first], d_ref[second]], axis=1)
        w = jnp.concatenate([w_ref[first], w_ref[second]], axis=1)
        ones.append(jnp.sum(gain * d, axis=1, keepdims=True))
        gain_hi, gain_lo = split(gain * (-0.5 * w))
        step = dot_nt(obs_hi, jnp.concatenate([gain_hi, gain_lo], axis=0))
        step = step[:, :BLK] + step[:, BLK:] + dot_nt(obs_lo, gain_hi)
        if pair == 0:
            acc_ref[...] = step
        else:
            acc_ref[...] += step
    shift = functools.reduce(jnp.add, ones)
    row = jnp.transpose(jnp.broadcast_to(shift, (BLK, BLK)))[:1]
    return cell + (acc_ref[...] + row)


def window_scratch(ob, members):
    return [
        pltpu.VMEM((3 * ob, members, BLK), jnp.bfloat16),
        pltpu.VMEM((3 * ob, members, BLK), jnp.bfloat16),
        pltpu.VMEM((3 * ob, 1, BLK), jnp.float32),
        pltpu.VMEM((3 * ob, 1, BLK), jnp.float32),
        pltpu.VMEM((members, BLK), jnp.float32),
    ]


def params(collective_id):
    return pltpu.CompilerParams(
        dimension_semantics=("arbitrary",),
        vmem_limit_bytes=56 * 1024 * 1024,
        collective_id=collective_id,
        has_side_effects=True,
    )


def cost(blocks, members, loc):
    return pl.CostEstimate(
        flops=16 * blocks * members * BLK * BLK * loc, bytes_accessed=32 << 20, transcendentals=0
    )


def first_kernel(nb, ob, loc, space_n, *refs):
    ints_ref, cell_ref, op_ref, reach_ref, tile_ref, picked_ref, cells_ref, table_ref = refs[:8]
    before_ref, own_ref, after_ref, values_ref, weights_ref, tiles_ref = refs[8:14]
    out_ref, obs_ref, prev_ref, next_ref = refs[14:18]
    scratch, (stage_ref, send_sem, recv_sem) = refs[18:23], refs[23:]
    n = pl.program_id(0)
    me = lax.axis_index("member")
    slab, after, before = ring_of_slabs(space_n)
    per_member = -(-2 * nb * loc // (8 * BLK)) * 8

    def side(block, way):
        return send(
            stage_ref.at[block],
            columns((prev_ref, next_ref)[way], block),
            send_sem.at[block, way],
            recv_sem.at[block, way],
            me,
            (after, before)[way],
        )

    @pl.when(n == 0)
    def _():
        barrier = pltpu.get_barrier_semaphore()
        for space in (after, before):
            pl.semaphore_signal(
                barrier, inc=1, device_id=(me, space), device_id_type=pl.DeviceIdType.MESH
            )
        pl.semaphore_wait(barrier, 2)
        load_window(0, ob, space_n, (before_ref, own_ref, after_ref), values_ref, weights_ref, scratch)

    @pl.when(n < ob)
    def _():
        cell = cell_ref[ob + n]
        owner = cell // nb

        def look(which, l):
            at = (which * nb + cell - owner * nb) * loc + l
            return ints_ref[owner * per_member + at // BLK, lax.rem(at, BLK)]

        picks = [(look(0, l), look(1, l)) for l in range(loc)]
        fresh_hi, fresh_lo = split(update(picked_ref[...], picks, tiles_ref, scratch))
        op_hi, op_lo = split(table_ref[op_ref[ob + n]])
        part = dot_nt(fresh_hi, jnp.concatenate([op_hi, op_lo], axis=0))
        part = part[:, :BLK] + part[:, BLK:] + dot_nt(fresh_lo, op_hi)
        obs_ref[...] = part
        stage_ref[n] = part
        side(n, 0).start()
        side(n, 1).start()

    @pl.when(n >= ob)
    def _():
        b = jnp.maximum(n - ob, 0)
        picks = [(reach_ref[b, l], tile_ref[b, l]) for l in range(loc)]
        out_ref[...] = update(cells_ref[...], picks, tiles_ref, scratch)

    @pl.when(n == ob + nb - 1)
    def _():
        for block in range(ob):
            side(block, 0).wait()
            side(block, 1).wait()


def first_batch(ints, cell, ops, reach, tile_pick, picked, cells, table, window, values, weights, tiles):
    members, wide = picked.shape
    nb, ob, loc = cells.shape[1] // BLK, wide // BLK, reach.shape[1]
    whole = pl.BlockSpec(memory_space=pltpu.VMEM)
    anywhere = pl.BlockSpec(memory_space=pl.ANY)
    early = pl.BlockSpec((members, BLK), lambda n, *_: (0, jnp.minimum(n, ob - 1)))
    late = pl.BlockSpec((members, BLK), lambda n, *_: (0, jnp.maximum(n - ob, 0)))
    seen = jax.ShapeDtypeStruct(picked.shape, jnp.float32)
    return pl.pallas_call(
        functools.partial(first_kernel, nb, ob, loc, lax.axis_size("space")),
        grid_spec=pltpu.PrefetchScalarGridSpec(
            num_scalar_prefetch=5,
            grid=(ob + nb,),
            in_specs=[early, late] + [whole] * 7,
            out_specs=[late, early, anywhere, anywhere],
            scratch_shapes=window_scratch(ob, members) + [
                pltpu.VMEM((ob, members, BLK), jnp.float32),
                pltpu.SemaphoreType.DMA((ob, 2)),
                pltpu.SemaphoreType.DMA((ob, 2)),
            ],
        ),
        out_shape=[jax.ShapeDtypeStruct(cells.shape, jnp.float32), seen, seen, seen],
        compiler_params=params(1),
        cost_estimate=cost(ob + nb, members, loc),
    )(ints, cell, ops, reach, tile_pick, picked, cells, table, *window, values, weights, tiles)


def last_kernel(nb, ob, loc, member_n, space_n, *refs):
    reach_ref, tile_ref, cells_ref, before_ref, own_ref, after_ref = refs[:6]
    values_ref, weights_ref, tiles_ref, out_ref = refs[6:10]
    scratch, (stage_ref, send_sem, recv_sem, local_sem) = refs[10:15], refs[15:]
    n = pl.program_id(0)
    me = lax.axis_index("member")
    slab = lax.axis_index("space")
    share = out_ref.shape[0]

    def part(block, member):
        return stage_ref.at[block, pl.ds(pl.multiple_of(member * share, 8), share)]

    def give(block, hop):
        peer = lax.rem(me + hop, member_n)
        return send(
            part(block, peer),
            columns(out_ref, me * nb + block),
            send_sem.at[block, hop],
            recv_sem.at[block, me],
            peer,
            slab,
        )

    def keep(block):
        return pltpu.make_async_copy(
            part(block, me), columns(out_ref, me * nb + block), local_sem.at[block]
        )

    @pl.when(n == 0)
    def _():
        barrier = pltpu.get_barrier_semaphore()
        for hop in range(1, member_n):
            peer = lax.rem(me + hop, member_n)
            pl.semaphore_signal(
                barrier, inc=1, device_id=(peer, slab), device_id_type=pl.DeviceIdType.MESH
            )
        pl.semaphore_wait(barrier, member_n - 1)
        load_window(1, ob, space_n, (before_ref, own_ref, after_ref), values_ref, weights_ref, scratch)

    picks = [(reach_ref[n, l], tile_ref[n, l]) for l in range(loc)]
    stage_ref[n] = update(cells_ref[...], picks, tiles_ref, scratch)
    for hop in range(1, member_n):
        give(n, hop).start()
    keep(n).start()

    @pl.when(n == nb - 1)
    def _():
        for block in range(nb):
            keep(block).wait()
            for hop in range(1, member_n):
                give(block, hop).wait_send()
                peer = lax.rem(me + hop, member_n)
                send(
                    part(block, peer),
                    columns(out_ref, peer * nb + block),
                    send_sem.at[block, hop],
                    recv_sem.at[block, peer],
                    peer,
                    slab,
                ).wait_recv()


def last_batch(reach, tile_pick, cells, window, values, weights, tiles):
    members, width = cells.shape
    nb, ob, loc = width // BLK, window[0].shape[1] // BLK, reach.shape[1]
    member_n = lax.axis_size("member")
    whole = pl.BlockSpec(memory_space=pltpu.VMEM)
    block = pl.BlockSpec((members, BLK), lambda n, *_: (0, n))
    return pl.pallas_call(
        functools.partial(last_kernel, nb, ob, loc, member_n, lax.axis_size("space")),
        grid_spec=pltpu.PrefetchScalarGridSpec(
            num_scalar_prefetch=2,
            grid=(nb,),
            in_specs=[block] + [whole] * 6,
            out_specs=pl.BlockSpec(memory_space=pl.ANY),
            scratch_shapes=window_scratch(ob, members) + [
                pltpu.VMEM((nb, members, BLK), jnp.float32),
                pltpu.SemaphoreType.DMA((nb, member_n)),
                pltpu.SemaphoreType.DMA((nb, member_n)),
                pltpu.SemaphoreType.DMA((nb,)),
            ],
        ),
        out_shape=jax.ShapeDtypeStruct((members // member_n, width * member_n), jnp.float32),
        compiler_params=params(2),
        cost_estimate=cost(nb, members, loc),
    )(reach, tile_pick, cells, *window, values, weights, tiles)


def pick_kernel(ob, cell_ref, op_ref, states_ref, op_block_ref, observed_ref, picked_ref):
    n = pl.program_id(0)

    @pl.when(n < ob)
    def _():
        observed_ref[...] = lax.dot_general(
            states_ref[...],
            op_block_ref[0],
            NT_DIMS,
            precision=lax.Precision.HIGHEST,
            preferred_element_type=jnp.float32,
        )

    @pl.when(n >= ob)
    def _():
        picked_ref[...] = states_ref[...]


def pick_blocks(cell, ops, states, table):
    share, ob = states.shape[0], cell.shape[0] // 2
    out = jax.ShapeDtypeStruct((share, ob * BLK), jnp.float32)
    return pl.pallas_call(
        functools.partial(pick_kernel, ob),
        grid_spec=pltpu.PrefetchScalarGridSpec(
            num_scalar_prefetch=2,
            grid=(2 * ob,),
            in_specs=[
                pl.BlockSpec((share, BLK), lambda n, cell, ops: (0, cell[n])),
                pl.BlockSpec((1, BLK, BLK), lambda n, cell, ops: (ops[n], 0, 0)),
            ],
            out_specs=[
                pl.BlockSpec((share, BLK), lambda n, *_: (0, jnp.minimum(n, ob - 1))),
                pl.BlockSpec((share, BLK), lambda n, *_: (0, jnp.maximum(n - ob, 0))),
            ],
        ),
        out_shape=[out, out],
    )(cell, ops, states, table)


def gather_kernel(member_n, space_n, *refs):
    ins, states_ref, refs = refs[:3], refs[3], refs[4:]
    outs, refs = refs[:3], refs[3:]
    prev_ref, next_ref, cells_ref, send_sem, recv_sem, halo_send, halo_recv, local_sem = refs[:8]
    swap_send, swap_recv = refs[8:]
    share, width = states_ref.shape[0], cells_ref.shape[1]
    me = lax.axis_index("member")
    slab = lax.axis_index("space")
    line = member_n // 2
    at, lane = me // 2, lax.rem(me, 2)
    mate = at * 2 + 1 - lane
    after = lax.rem(slab + 1, space_n)
    before = lax.rem(slab + space_n - 1, space_n)

    barrier = pltpu.get_barrier_semaphore()

    def greet(member, space):
        pl.semaphore_signal(
            barrier, inc=1, device_id=(member, space), device_id_type=pl.DeviceIdType.MESH
        )

    greet(me, after)
    greet(me, before)
    for hop_by in range(1, member_n):
        greet(lax.rem(me + hop_by, member_n), slab)
    pl.semaphore_wait(barrier, member_n + 1)

    def states_for(member):
        return states_ref.at[:, pl.ds(pl.multiple_of(member * width, BLK), width)]

    def cells_of(member):
        return cells_ref.at[pl.ds(pl.multiple_of(member * share, 8), share)]

    def swap(hop_by):
        peer = lax.rem(me + hop_by, member_n)
        return send(
            states_for(peer), cells_of(me), swap_send.at[hop_by], swap_recv.at[me], peer, slab
        )

    hops = sorted(range(1, member_n), key=lambda k: (abs(k - line), k))
    each = -(-len(hops) // line)

    def swaps(step):
        for hop_by in hops[step * each:(step + 1) * each]:
            swap(hop_by).start()

    def rows(ref, item, block):
        size = ins[item].shape[0]
        return ref.at[pl.ds(pl.multiple_of(block * size, 8), size)]

    def hop(item, block, way, target, mine=False):
        return pltpu.make_async_remote_copy(
            src_ref=ins[item] if mine else rows(outs[item], item, block),
            dst_ref=rows(outs[item], item, block),
            send_sem=send_sem.at[item, block, way],
            recv_sem=recv_sem.at[item, block],
            device_id=(target, slab),
            device_id_type=pl.DeviceIdType.MESH,
        )

    def side(block, way, mine=False):
        return pltpu.make_async_remote_copy(
            src_ref=ins[0] if mine else rows(outs[0], 0, block),
            dst_ref=rows((prev_ref, next_ref)[way], 0, block),
            send_sem=halo_send.at[block, way],
            recv_sem=halo_recv.at[block, way],
            device_id=(me, (after, before)[way]),
            device_id_type=pl.DeviceIdType.MESH,
        )

    def sides(block, mine=False):
        side(block, 0, mine).start()
        side(block, 1, mine).start()

    for item in range(3):
        @pl.when(at < line - 1)
        def _():
            hop(item, me, 0, me + 2, True).start()

        @pl.when(at > 0)
        def _():
            hop(item, me, 1, me - 2, True).start()

        hop(item, me, 2, mate, True).start()
    sides(me, True)
    local = [
        pltpu.make_async_copy(ins[item], rows(outs[item], item, me), local_sem.at[item])
        for item in range(3)
    ]
    kept = pltpu.make_async_copy(states_for(me), cells_of(me), local_sem.at[3])
    swaps(0)
    for copy in local + [kept]:
        copy.start()

    def landed(item, block):
        hop(item, block, 2, mate).wait_recv()

    def from_mate(block):
        for item in range(3):
            landed(item, block)
            if item == 0:
                sides(block)

    for step in range(1, line):
        low, high = me - 2 * step, me + 2 * step

        @pl.when(low >= 0)
        def _():
            for item in range(3):
                landed(item, low)

                @pl.when(at < line - 1)
                def _():
                    hop(item, low, 0, me + 2).start()

                hop(item, low, 2, mate).start()
                if item == 0:
                    sides(low)

        @pl.when(high < member_n)
        def _():
            for item in range(3):
                landed(item, high)

                @pl.when(at > 0)
                def _():
                    hop(item, high, 1, me - 2).start()

                hop(item, high, 2, mate).start()
                if item == 0:
                    sides(high)

        swaps(step)
        if step == 1:
            from_mate(mate)
        else:
            @pl.when(mate - 2 * (step - 1) >= 0)
            def _():
                from_mate(mate - 2 * (step - 1))

            @pl.when(mate + 2 * (step - 1) < member_n)
            def _():
                from_mate(mate + 2 * (step - 1))

    @pl.when(mate - 2 * (line - 1) >= 0)
    def _():
        from_mate(mate - 2 * (line - 1))

    @pl.when(mate + 2 * (line - 1) < member_n)
    def _():
        from_mate(mate + 2 * (line - 1))

    for copy in local + [kept]:
        copy.wait()
    for hop_by in range(1, member_n):
        swap(hop_by).wait_send()
        peer = lax.rem(me + hop_by, member_n)
        send(
            states_for(peer), cells_of(peer), swap_send.at[hop_by], swap_recv.at[peer], peer, slab
        ).wait_recv()
    for block in range(member_n):
        for way in range(2):
            side(block, way).wait()
        place, same = block // 2, block % 2 == lane
        for item in range(3):
            @pl.when(same & (place <= at) & (at < line - 1))
            def _():
                hop(item, block, 0, mate).wait_send()

            @pl.when(same & (place >= at) & (at > 0))
            def _():
                hop(item, block, 1, mate).wait_send()

            @pl.when(same)
            def _():
                hop(item, block, 2, mate).wait_send()


def gather(observed, picked, ints, states):
    member_n, space_n = lax.axis_size("member"), lax.axis_size("space")
    parts = (observed, picked, ints)
    out = [jax.ShapeDtypeStruct((member_n * a.shape[0], a.shape[1]), a.dtype) for a in parts]
    share, width = states.shape
    cells = jax.ShapeDtypeStruct((share * member_n, width // member_n), states.dtype)
    return pl.pallas_call(
        functools.partial(gather_kernel, member_n, space_n),
        out_shape=out + [out[0], out[0], cells],
        in_specs=[pl.BlockSpec(memory_space=pltpu.VMEM)] * 3 + [pl.BlockSpec(memory_space=pl.ANY)],
        out_specs=[pl.BlockSpec(memory_space=pl.ANY)] * 6,
        scratch_shapes=[
            pltpu.SemaphoreType.DMA((3, member_n, 3)),
            pltpu.SemaphoreType.DMA((3, member_n)),
            pltpu.SemaphoreType.DMA((member_n, 2)),
            pltpu.SemaphoreType.DMA((member_n, 2)),
            pltpu.SemaphoreType.DMA((4,)),
            pltpu.SemaphoreType.DMA((member_n,)),
            pltpu.SemaphoreType.DMA((member_n,)),
        ],
        compiler_params=pltpu.CompilerParams(collective_id=0, has_side_effects=True),
    )(*parts, states)


def per_device(
    states, obs_values, obs_weights, obs_cell, op_select, op_table, loc_obs, loc_tile, loc_tiles
):
    nb, loc = loc_obs.shape[2:]
    cell, ops = obs_cell.reshape(-1), op_select.reshape(-1)
    values = obs_values.reshape(-1, 1, BLK)
    weights = obs_weights.reshape(-1, 1, BLK)
    ints = jnp.concatenate([loc_obs[0, 0], loc_tile[0, 0]]).reshape(-1)
    extra = -(-ints.shape[0] // (8 * BLK)) * 8
    ints = jnp.pad(ints, (0, extra * BLK - ints.shape[0])).reshape(extra, BLK)

    observed, picked = pick_blocks(cell, ops, states, op_table)
    own, picked, ints, before, after, cells = gather(observed, picked, ints, states)
    cells, own, before, after = first_batch(
        ints, cell, ops, loc_obs[0, 0], loc_tile[0, 0], picked, cells, op_table,
        (before, own, after), values, weights, loc_tiles,
    )
    return last_batch(
        loc_obs[1, 0], loc_tile[1, 0], cells, (before, own, after), values, weights, loc_tiles
    )


def solution(mesh):
    placed = (
        P("member", "space"),
        P(),
        P(),
        P(None, "space", None),
        P(None, "space", None),
        P(),
        P(None, "space", "member", None),
        P(None, "space", "member", None),
        P(),
    )
    return jax.shard_map(
        per_device, mesh=mesh, in_specs=placed, out_specs=P("member", "space"), check_vma=False
    )
```

profile of v0, /device:TPU:0, one launch (start us, length us, event | category | flops | bytes accessed | tf_op | source)
XLA Modules:
  0.0 270.1 jit_solution(9675759638695607974)
XLA Ops:
  0.0 0.5 broadcast.8
  0.5 1.3 reduce.6
  1.9 0.7 reshape.18.cell_ref.refs_1_
  2.5 1.3 reduce.7
  3.9 0.7 reshape.19.op_ref.refs_2_
  4.5 0.7 fusion
  5.2 0.6 copy_bitcast_fusion.1
  5.8 0.0 copy-start
  5.8 0.7 fusion.1
  6.5 0.6 copy_bitcast_fusion
  7.1 0.0 copy-start.1
  7.1 0.1 reshape.20
  7.2 0.6 pad_bitcast_fusion.refs_2_
  7.8 1.3 reshape.22.refs_11_.refs_6_
  9.2 1.3 reshape.23.refs_12_.refs_7_
  10.5 6.1 %shard_map.91 = (f32[128,512]{1,0:T(8,128)}, f32[128,512]{1,0:T(8,128)}) custom-call(s32[8]{0:T(128)} %reshape.18.cell_ref.refs_1_, s32[8]{0:T(128)} %reshape.19.op_ref.refs_2_, f32[128,6144]{1,0:T(8,128)} %refs_3_.1, f32[8,128,128]{2,1,0:T(8,128)} %refs_7_.1), custom_call_target="tpu_custom_call" | custom-call | tf_op jit(solution)/shard_map/pallas_call | solution.py:319
  16.6 104.4 %shard_map.92 = (f32[1024,512]{1,0:T(8,128)}, f32[1024,512]{1,0:T(8,128)}, s32[64,128]{1,0:T(8,128)}, f32[1024,512]{1,0:T(8,128)}, f32[1024,512]{1,0:T(8,128)}, /*index=5*/f32[1024,768]{1,0:T(8,128)}) custom-call(f32[128,512]{1,0:T(8,128)} %get-tuple-element.17.refs_0_, f32[128,512]{1,0:T(8,128)} %get-tuple-element.18.refs_1_, ...), custom_call_target="tpu_custom_call" | custom-call | tf_op jit(solution)/shard_map/pallas_call | solution.py:521
  121.0 0.0 copy-done
  121.0 0.0 copy-done.1
  121.0 59.0 %shard_map.93 = (f32[1024,768]{1,0:T(8,128)}, f32[1024,512]{1,0:T(8,128)}, f32[1024,512]{1,0:T(8,128)}, f32[1024,512]{1,0:T(8,128)}) custom-call(s32[64,128]{1,0:T(8,128)} %get-tuple-element.19.refs_0_, s32[8]{0:T(128)} %reshape.18.cell_ref.refs_1_, s32[8]{0:T(128)} %reshape.19.op_ref.refs_2_, s32[6,8]{1,0:T(8,128)} %copy-done, s32[6,8]{1,0:T(8,128)} %copy-done.1, ...), custom_call_target="tpu_custom_call" | custom-call | flops 21474836480 | bytes 33554432 | tf_op jit(solution)/shard_map/pallas_call | solution.py:191
  180.1 86.2 %shard_map.94 = f32[128,6144]{1,0:T(8,128)} custom-call(s32[6,8]{1,0:T(8,128)} %get-tuple-element.34.refs_0_, s32[6,8]{1,0:T(8,128)} %get-tuple-element.36.refs_1_, f32[1024,768]{1,0:T(8,128)} %get-tuple-element.25.refs_2_, f32[1024,512]{1,0:T(8,128)} %get-tuple-element.26.refs_3_, f32[1024,512]{1,0:T(8,128)} %get-tuple-element.27.refs_4_, ...), custom_call_target="tpu_custom_call" | custom-call | flops 12884901888 | bytes 33554432 | tf_op jit(solution)/shard_map/pallas_call | solution.py:278
  266.2 3.9 %copy.27 = f32[128,6144]{1,0:T(8,128)} copy(f32[128,6144]{1,0:T(8,128)} %shard_map.94) | data formatting | bytes 6291456
  (1 shorter events, 0.0 us)
Async XLA Ops:
  5.8 115.2 %copy-start = (s32[6,8]{1,0:T(8,128)}, s32[6,8]{1,0:T(8,128)S(1)}, u32[]{:S(2)}) copy-start(s32[6,8]{1,0:T(8,128)S(1)} %get-tuple-element.33.refs_3_) | copy-start | bytes 580
  7.1 113.9 %copy-start.1 = (s32[6,8]{1,0:T(8,128)}, s32[6,8]{1,0:T(8,128)S(1)}, u32[]{:S(2)}) copy-start(s32[6,8]{1,0:T(8,128)S(1)} %get-tuple-element.35.refs_4_) | copy-start | bytes 580
where the time goes:
time: 272 us; the launch traced here: 270 us
  Pallas kernels  256 us (94%)
  local copies, waits for them, and re-layouts  11.7 us (4%)
    pallas_call x1, Pallas kernels, gather(): pl.pallas_call(functools.partial(gather_kernel, member_n, space_n), out_s...  104 us
    pallas_call x1, Pallas kernels, last_batch(): pl.pallas_call(functools.partial(last_kernel, nb, ob, loc, member_n, lax....  86.2 us
    pallas_call x1, Pallas kernels, first_batch(): pl.pallas_call(functools.partial(first_kernel, nb, ob, loc, lax.axis_size...  59 us
    pallas_call x1, Pallas kernels, pick_blocks(): pl.pallas_call(functools.partial(pick_kernel, ob), grid_spec=pltpu.Prefet...  6.06 us

commit v1 on v0

v1 whole, which is shorter than its diff:
```python
import functools

import jax
import jax.numpy as jnp
from jax import lax
from jax.experimental import pallas as pl
from jax.experimental.pallas import tpu as pltpu
from jax.sharding import PartitionSpec as P

BLK = 128
NT_DIMS = (((1,), (1,)), ((), ()))


def split(x):
    hi = x.astype(jnp.bfloat16)
    lo = (x - hi.astype(jnp.float32)).astype(jnp.bfloat16)
    return hi, lo


def dot(a, b):
    return jnp.dot(a, b, preferred_element_type=jnp.float32)


def dot_nt(a, b):
    return lax.dot_general(a, b, NT_DIMS, preferred_element_type=jnp.float32)


def observe(block, operator):
    hi, lo = split(block)
    op_hi, op_lo = split(operator)
    part = dot_nt(hi, jnp.concatenate([op_hi, op_lo], axis=0))
    return part[:, :BLK] + part[:, BLK:] + dot_nt(lo, op_hi)


def send(src, dst, send_sem, recv_sem, member, space):
    return pltpu.make_async_remote_copy(
        src_ref=src,
        dst_ref=dst,
        send_sem=send_sem,
        recv_sem=recv_sem,
        device_id=(member, space),
        device_id_type=pl.DeviceIdType.MESH,
    )


def columns(ref, block):
    return ref.at[:, pl.ds(pl.multiple_of(block * BLK, BLK), BLK)]


def load_window(batch, place, source, window_ref, values_ref, weights_ref, scratch):
    hi_ref, lo_ref, d_ref, w_ref = scratch[:4]
    _, ob, members, _ = window_ref.shape
    for o in range(ob):
        j = place * ob + o
        at = pl.ds(pl.multiple_of((source * ob + o) * BLK, BLK), BLK)
        weight = weights_ref[batch:batch + 1, at]
        block = window_ref[place, o]
        mean = jnp.sum(block, axis=0, keepdims=True) * (1.0 / members)
        hi, lo = split(block - mean)
        hi_ref[j] = hi
        lo_ref[j] = lo
        w_ref[j] = weight
        d_ref[j] = weight * (values_ref[batch:batch + 1, at] - mean)


def update(cell, picks, tiles_ref, scratch, acc_ref):
    hi_ref, lo_ref, d_ref, w_ref = scratch
    members = cell.shape[0]
    mean = jnp.sum(cell, axis=0, keepdims=True) * (1.0 / members)
    hi, lo = split(jnp.transpose(cell - mean))
    both = jnp.concatenate([hi, lo], axis=0)
    ones = []
    for pair in range(len(picks) // 2):
        (first, tile_a), (second, tile_b) = picks[2 * pair], picks[2 * pair + 1]
        obs_hi = jnp.concatenate([hi_ref[first], hi_ref[second]], axis=1)
        obs_lo = jnp.concatenate([lo_ref[first], lo_ref[second]], axis=1)
        part = dot(both, obs_hi)
        cov = part[:BLK] + part[BLK:] + dot(hi, obs_lo)
        tile = jnp.concatenate([tiles_ref[tile_a], tiles_ref[tile_b]], axis=1)
        gain = tile * (cov * (1.0 / (members - 1)))
        d = jnp.concatenate([d_ref[first], d_ref[second]], axis=1)
        w = jnp.concatenate([w_ref[first], w_ref[second]], axis=1)
        ones.append(jnp.sum(gain * d, axis=1, keepdims=True))
        gain_hi, gain_lo = split(gain * (-0.5 * w))
        step = dot_nt(obs_hi, jnp.concatenate([gain_hi, gain_lo], axis=0))
        step = step[:, :BLK] + step[:, BLK:] + dot_nt(obs_lo, gain_hi)
        if pair == 0:
            acc_ref[...] = step
        else:
            acc_ref[...] += step
    shift = functools.reduce(jnp.add, ones)
    row = jnp.transpose(jnp.broadcast_to(shift, (BLK, BLK)))[:1]
    return cell + (acc_ref[...] + row)


def kernel(member_n, space_n, *refs):
    cell_ref, op_ref, reach_ref, tile_ref, reach_src, tile_src = refs[:6]
    states_hbm, values_ref, weights_ref, table_ref, tiles_ref, out_ref = refs[6:12]
    states_ref, cells_ref, picks_ref, win1_ref, win2_ref, acc_ref = refs[12:18]
    ints_ref, table_of_ints, scratch1, scratch2 = refs[18], refs[19], refs[20:24], refs[24:28]
    load_sem, local_sem, ints_send, ints_recv, hop_send, hop_recv, halo_send, halo_recv = refs[28:36]
    in_send, in_recv, in_local, back_send, back_recv, out_send, out_recv, out_local = refs[36:]

    nb, members, _ = cells_ref.shape
    ob, loc = picks_ref.shape[0], reach_ref.shape[3]
    share = states_ref.shape[1]
    me = lax.axis_index("member")
    slab = lax.axis_index("space")
    after = lax.rem(slab + 1, space_n)
    before = lax.rem(slab + space_n - 1, space_n)
    line = member_n // 2
    at, lane = me // 2, lax.rem(me, 2)
    mate = at * 2 + 1 - lane

    def load(block):
        return pltpu.make_async_copy(
            columns(states_hbm, block), states_ref.at[block], load_sem.at[block]
        )

    @pl.loop(0, member_n * nb)
    def _(block):
        load(block).start()

    barrier = pltpu.get_barrier_semaphore()

    def greet(member, space):
        pl.semaphore_signal(
            barrier, inc=1, device_id=(member, space), device_id_type=pl.DeviceIdType.MESH
        )

    greet(me, after)
    greet(me, before)
    for hop_by in range(1, member_n):
        greet(lax.rem(me + hop_by, member_n), slab)

    def rows(member):
        return pl.ds(pl.multiple_of(member * share, 8), share)

    @pl.loop(0, member_n * nb)
    def _(block):
        load(block).wait()

    own_ref = win1_ref.at[1]
    for o in range(ob):
        own_ref[o, rows(me)] = observe(states_ref[cell_ref[0, 0, o]], table_ref[op_ref[0, 0, o]])
    for o in range(ob):
        picks_ref[o, rows(me)] = states_ref[cell_ref[1, 0, o]]
    pl.semaphore_wait(barrier, member_n + 1)

    def hop(item, member, way, target):
        part = (own_ref, picks_ref)[item].at[:, rows(member)]
        return send(
            part, part, hop_send.at[item, member, way], hop_recv.at[item, member], target, slab
        )

    def side(member, way):
        return send(
            own_ref.at[:, rows(member)],
            win1_ref.at[2 * way, :, rows(member)],
            halo_send.at[member, way],
            halo_recv.at[member, way],
            me,
            (after, before)[way],
        )

    def pass_on(item, member, up, down, across):
        if up:
            @pl.when(at < line - 1)
            def _():
                hop(item, member, 0, me + 2).start()

        if down:
            @pl.when(at > 0)
            def _():
                hop(item, member, 1, me - 2).start()

        if across:
            hop(item, member, 2, mate).start()
        if item == 0:
            side(member, 0).start()
            side(member, 1).start()

    def landed(item, member):
        hop(item, member, 2, mate).wait_recv()

    def take(block, hop_by):
        peer = lax.rem(me + hop_by, member_n)
        return send(
            states_ref.at[peer * nb + block],
            cells_ref.at[block, rows(me)],
            in_send.at[block, hop_by],
            in_recv.at[block, me],
            peer,
            slab,
        )

    def stay(block):
        return pltpu.make_async_copy(
            states_ref.at[me * nb + block], cells_ref.at[block, rows(me)], in_local.at[block]
        )

    hops = sorted(range(1, member_n), key=lambda k: (abs(k - line), k))

    def swap_in(block):
        for hop_by in hops:
            take(block, hop_by).start()
        stay(block).start()

    def give_ints(which, hop_by):
        peer = lax.rem(me + hop_by, member_n)
        return send(
            (reach_src, tile_src)[which].at[0, 0],
            ints_ref.at[which, me],
            ints_send.at[which, hop_by],
            ints_recv.at[which, me],
            peer,
            slab,
        )

    def keep_ints(which):
        return pltpu.make_async_copy(
            (reach_src, tile_src)[which].at[0, 0], ints_ref.at[which, me], local_sem.at[1 + which]
        )

    pass_on(0, me, True, True, True)
    for which in range(2):
        for hop_by in range(1, member_n):
            give_ints(which, hop_by).start()
        keep_ints(which).start()
    pass_on(1, me, True, True, True)
    swap_in(0)

    for item in range(2):
        for step in range(1, line):
            low, high = me - 2 * step, me + 2 * step

            @pl.when(low >= 0)
            def _():
                landed(item, low)
                pass_on(item, low, True, False, True)

            @pl.when(high < member_n)
            def _():
                landed(item, high)
                pass_on(item, high, False, True, True)

            far = 2 * (step - 1)
            if far == 0:
                landed(item, mate)
                pass_on(item, mate, False, False, False)
            else:
                @pl.when(mate - far >= 0)
                def _():
                    landed(item, mate - far)
                    pass_on(item, mate - far, False, False, False)

                @pl.when(mate + far < member_n)
                def _():
                    landed(item, mate + far)
                    pass_on(item, mate + far, False, False, False)

        far = 2 * (line - 1)

        @pl.when(mate - far >= 0)
        def _():
            landed(item, mate - far)
            pass_on(item, mate - far, False, False, False)

        @pl.when(mate + far < member_n)
        def _():
            landed(item, mate + far)
            pass_on(item, mate + far, False, False, False)

        if item == 0:
            swap_in(1)

    @pl.loop(2, nb)
    def _(block):
        swap_in(block)

    for which in range(2):
        keep_ints(which).wait()
        for hop_by in range(1, member_n):
            peer = lax.rem(me + hop_by, member_n)
            send(
                (reach_src, tile_src)[which].at[0, 0],
                ints_ref.at[which, peer],
                ints_send.at[which, hop_by],
                ints_recv.at[which, peer],
                peer,
                slab,
            ).wait_recv()
    scalars = pltpu.make_async_copy(ints_ref, table_of_ints, local_sem.at[3])
    scalars.start()

    near = 2 * (1 - lax.rem(slab, 2))
    far = 2 - near

    def source_of(place):
        return lax.rem(slab + space_n - 1 + place, space_n)

    load_window(0, 1, slab, win1_ref, values_ref, weights_ref, scratch1)
    for way in range(2):
        for member in range(member_n):
            side(member, way).wait_recv()
    for place in (near, far):
        load_window(0, place, source_of(place), win1_ref, values_ref, weights_ref, scratch1)
    scalars.wait()

    def back(o, way):
        return send(
            win2_ref.at[1, o],
            win2_ref.at[2 * way, o],
            back_send.at[o, way],
            back_recv.at[o, way],
            me,
            (after, before)[way],
        )

    @pl.loop(0, ob)
    def _(o):
        cell = cell_ref[1, 0, o]
        owner = cell // nb
        place = cell - owner * nb
        picks = [
            (table_of_ints[0, owner, place, l], table_of_ints[1, owner, place, l])
            for l in range(loc)
        ]
        fresh = update(picks_ref[o], picks, tiles_ref, scratch1, acc_ref)
        win2_ref[1, o] = observe(fresh, table_ref[op_ref[1, 0, o]])
        back(o, 0).start()
        back(o, 1).start()

    @pl.loop(0, nb)
    def _(block):
        stay(block).wait()
        for hop_by in range(1, member_n):
            peer = lax.rem(me + hop_by, member_n)
            send(
                states_ref.at[peer * nb + block],
                cells_ref.at[block, rows(peer)],
                in_send.at[block, hop_by],
                in_recv.at[block, peer],
                peer,
                slab,
            ).wait_recv()
        picks = [(reach_ref[0, 0, block, l], tile_ref[0, 0, block, l]) for l in range(loc)]
        cells_ref[block] = update(cells_ref[block], picks, tiles_ref, scratch1, acc_ref)

    load_window(1, 1, slab, win2_ref, values_ref, weights_ref, scratch2)
    for way in range(2):
        for o in range(ob):
            back(o, way).wait_recv()
    for place in (near, far):
        load_window(1, place, source_of(place), win2_ref, values_ref, weights_ref, scratch2)

    def give(block, hop_by):
        peer = lax.rem(me + hop_by, member_n)
        return send(
            cells_ref.at[block, rows(peer)],
            columns(out_ref, me * nb + block),
            out_send.at[block, hop_by],
            out_recv.at[block, me],
            peer,
            slab,
        )

    def keep(block):
        return pltpu.make_async_copy(
            cells_ref.at[block, rows(me)], columns(out_ref, me * nb + block), out_local.at[block]
        )

    @pl.loop(0, nb)
    def _(block):
        picks = [(reach_ref[1, 0, block, l], tile_ref[1, 0, block, l]) for l in range(loc)]
        cells_ref[block] = update(cells_ref[block], picks, tiles_ref, scratch2, acc_ref)
        for hop_by in hops:
            give(block, hop_by).start()
        keep(block).start()

    for which in range(2):
        for hop_by in range(1, member_n):
            give_ints(which, hop_by).wait_send()
    for member in range(member_n):
        spot, same = member // 2, lane == member % 2
        for way in range(2):
            side(member, way).wait_send()
        for item in range(2):
            @pl.when(same & (spot <= at) & (at < line - 1))
            def _():
                hop(item, member, 0, mate).wait_send()

            @pl.when(same & (spot >= at) & (at > 0))
            def _():
                hop(item, member, 1, mate).wait_send()

            @pl.when(same)
            def _():
                hop(item, member, 2, mate).wait_send()
    for o in range(ob):
        for way in range(2):
            back(o, way).wait_send()

    @pl.loop(0, nb)
    def _(block):
        keep(block).wait()
        for hop_by in range(1, member_n):
            take(block, hop_by).wait_send()
            give(block, hop_by).wait_send()
            peer = lax.rem(me + hop_by, member_n)
            send(
                cells_ref.at[block, rows(peer)],
                columns(out_ref, peer * nb + block),
                out_send.at[block, hop_by],
                out_recv.at[block, peer],
                peer,
                slab,
            ).wait_recv()


def per_device(
    states, obs_values, obs_weights, obs_cell, op_select, op_table, loc_obs, loc_tile, loc_tiles
):
    member_n, space_n = lax.axis_size("member"), lax.axis_size("space")
    share, width = states.shape
    members = share * member_n
    ob = obs_cell.shape[2]
    nb, loc = loc_obs.shape[2:]
    f32, bf16, i32 = jnp.float32, jnp.bfloat16, jnp.int32
    smem = pl.BlockSpec(memory_space=pltpu.SMEM)
    vmem = pl.BlockSpec(memory_space=pltpu.VMEM)
    anywhere = pl.BlockSpec(memory_space=pl.ANY)
    dma = pltpu.SemaphoreType.DMA
    parts = [
        pltpu.VMEM((3 * ob, members, BLK), bf16),
        pltpu.VMEM((3 * ob, members, BLK), bf16),
        pltpu.VMEM((3 * ob, 1, BLK), f32),
        pltpu.VMEM((3 * ob, 1, BLK), f32),
    ]
    return pl.pallas_call(
        functools.partial(kernel, member_n, space_n),
        out_shape=jax.ShapeDtypeStruct((share, width), f32),
        in_specs=[smem] * 4 + [vmem] * 2 + [anywhere] + [vmem] * 4,
        out_specs=anywhere,
        scratch_shapes=[
            pltpu.VMEM((width // BLK, share, BLK), f32),
            pltpu.VMEM((nb, members, BLK), f32),
            pltpu.VMEM((ob, members, BLK), f32),
            pltpu.VMEM((3, ob, members, BLK), f32),
            pltpu.VMEM((3, ob, members, BLK), f32),
            pltpu.VMEM((members, BLK), f32),
            pltpu.VMEM((2, member_n, nb, loc), i32),
            pltpu.SMEM((2, member_n, nb, loc), i32),
        ] + parts + parts + [
            dma((width // BLK,)),
            dma((4,)),
            dma((2, member_n)),
            dma((2, member_n)),
            dma((2, member_n, 3)),
            dma((2, member_n)),
            dma((member_n, 2)),
            dma((member_n, 2)),
            dma((nb, member_n)),
            dma((nb, member_n)),
            dma((nb,)),
            dma((ob, 2)),
            dma((ob, 2)),
            dma((nb, member_n)),
            dma((nb, member_n)),
            dma((nb,)),
        ],
        compiler_params=pltpu.CompilerParams(
            vmem_limit_bytes=58 * 1024 * 1024, collective_id=0, has_side_effects=True
        ),
    )(
        obs_cell, op_select, loc_obs, loc_tile, loc_obs, loc_tile,
        states, obs_values, obs_weights, op_table, loc_tiles,
    )


def solution(mesh):
    placed = (
        P("member", "space"),
        P(),
        P(),
        P(None, "space", None),
        P(None, "space", None),
        P(),
        P(None, "space", "member", None),
        P(None, "space", "member", None),
        P(),
    )
    return jax.shard_map(
        per_device, mesh=mesh, in_specs=placed, out_specs=P("member", "space"), check_vma=False
    )
```

time: 272 us -> 199 us (0.73)
  Pallas kernels: 256 us -> 190 us
  local copies, waits for them, and re-layouts: 11.7 us -> 6.43 us
    pallas_call x4 -> x1, Pallas kernels: 256 us -> 190 us  [per_device(): pl.pallas_call(functools.partial(kernel, member_n, space_n), out_shape=ja...]
    reshape x6 -> x0, local copies, waits for them, and re-layouts: 4.7 us -> none  [the longest x1 1.35 us: per_device(): values = obs_values.reshape(-1, 1, BLK)]
    unnamed x6 -> x3, local copies, waits for them, and re-layouts: 4.37 us -> 6.43 us
where the time goes in v1:
time: 199 us; the launch traced here: 197 us
  Pallas kernels  190 us (95%)
  local copies, waits for them, and re-layouts  6.43 us (3%)
    pallas_call x1, Pallas kernels, per_device(): pl.pallas_call(functools.partial(kernel, member_n, space_n), out_shape=ja...  190 us
    unnamed x3, local copies, waits for them, and re-layouts  6.43 us

profile of v1, /device:TPU:0, one launch (start us, length us, event | category | flops | bytes accessed | tf_op | source)
XLA Modules:
  0.0 196.6 jit_solution(13516286396351683629)
XLA Ops:
  0.0 1.3 copy.10.refs_2_.refs_4_
  1.3 1.3 copy.11.refs_3_.refs_5_
  2.6 190.1 %shard_map.91 = f32[128,6144]{1,0:T(8,128)} custom-call(s32[2,1,4]{2,1,0:T(1,128)} %refs_0_.1, s32[2,1,4]{2,1,0:T(1,128)} %refs_1_.1, s32[2,1,6,8]{3,2,1,0:T(8,128)} %copy.10.refs_2_.refs_4_, s32[2,1,6,8]{3,2,1,0:T(8,128)} %copy.11.refs_3_.refs_5_, s32[2,1,6,8]{3,2,1,0:T(8,128)} %copy.10.refs_2_.refs_4_, s32[2,1,6,8]{3,2,1,0:T(8,128)} %copy.11.refs_3_.refs_5_, ...), custom_call_target="tpu_custom_call" | custom-call | tf_op jit(solution)/shard_map/pallas_call | solution.py:440
  192.7 3.9 %copy.15 = f32[128,6144]{1,0:T(8,128)} copy(f32[128,6144]{1,0:T(8,128)} %shard_map.91) | data formatting | bytes 6291456

commit v2 on v1

--- a/solution.py
+++ b/solution.py
@@ -201,10 +201,16 @@
 
     hops = sorted(range(1, member_n), key=lambda k: (abs(k - line), k))
 
-    def swap_in(block):
+    def straight(block):
         for hop_by in hops:
-            take(block, hop_by).start()
+            if hop_by % 2 == 0:
+                take(block, hop_by).start()
         stay(block).start()
+
+    def crossing(block):
+        for hop_by in hops:
+            if hop_by % 2 == 1:
+                take(block, hop_by).start()
 
     def give_ints(which, hop_by):
         peer = lax.rem(me + hop_by, member_n)
@@ -228,7 +234,7 @@
             give_ints(which, hop_by).start()
         keep_ints(which).start()
     pass_on(1, me, True, True, True)
-    swap_in(0)
+    straight(0)
 
     for item in range(2):
         for step in range(1, line):
@@ -244,6 +250,9 @@
                 landed(item, high)
                 pass_on(item, high, False, True, True)
 
+            if step == 1:
+                for b in ([1],[3])[item]:
+                    straight(b)
             far = 2 * (step - 1)
             if far == 0:
                 landed(item, mate)
@@ -272,11 +281,13 @@
             pass_on(item, mate + far, False, False, False)
 
         if item == 0:
-            swap_in(1)
-
-    @pl.loop(2, nb)
-    def _(block):
-        swap_in(block)
+            pass
+            straight(2)
+
+    for block in range(4, nb):
+        straight(block)
+    for block in range(nb):
+        crossing(block)
 
     for which in range(2):
         keep_ints(which).wait()

time: 199 us -> 193 us (0.970); the launches traced: 197 us -> 193 us
  Pallas kernels: 190 us -> 187 us
    pallas_call x1, Pallas kernels: 190 us -> 187 us  [per_device(): pl.pallas_call(functools.partial(kernel, member_n, space_n), out_shape=ja...]
where the time goes in v2:
time: 193 us
  Pallas kernels  187 us (97%)
  local copies, waits for them, and re-layouts  6.43 us (3%)
    pallas_call x1, Pallas kernels, per_device(): pl.pallas_call(functools.partial(kernel, member_n, space_n), out_shape=ja...  187 us
    unnamed x3, local copies, waits for them, and re-layouts  6.43 us

profile of v2, /device:TPU:0, one launch (start us, length us, event | category | flops | bytes accessed | tf_op | source)
XLA Modules:
  0.0 193.1 jit_solution(12117910326334786061)
XLA Ops:
  0.0 1.3 copy.10.refs_2_.refs_4_
  1.3 1.3 copy.11.refs_3_.refs_5_
  2.6 186.6 %shard_map.91 = f32[128,6144]{1,0:T(8,128)} custom-call(s32[2,1,4]{2,1,0:T(1,128)} %refs_0_.1, s32[2,1,4]{2,1,0:T(1,128)} %refs_1_.1, s32[2,1,6,8]{3,2,1,0:T(8,128)} %copy.10.refs_2_.refs_4_, s32[2,1,6,8]{3,2,1,0:T(8,128)} %copy.11.refs_3_.refs_5_, s32[2,1,6,8]{3,2,1,0:T(8,128)} %copy.10.refs_2_.refs_4_, s32[2,1,6,8]{3,2,1,0:T(8,128)} %copy.11.refs_3_.refs_5_, ...), custom_call_target="tpu_custom_call" | custom-call | tf_op jit(solution)/shard_map/pallas_call | solution.py:451
  189.2 3.9 %copy.15 = f32[128,6144]{1,0:T(8,128)} copy(f32[128,6144]{1,0:T(8,128)} %shard_map.91) | data formatting | bytes 6291456

commit v3 on v2

--- a/solution.py
+++ b/solution.py
@@ -93,17 +93,22 @@
     return cell + (acc_ref[...] + row)
 
 
-def kernel(member_n, space_n, *refs):
-    cell_ref, op_ref, reach_ref, tile_ref, reach_src, tile_src = refs[:6]
-    states_hbm, values_ref, weights_ref, table_ref, tiles_ref, out_ref = refs[6:12]
-    states_ref, cells_ref, picks_ref, win1_ref, win2_ref, acc_ref = refs[12:18]
-    ints_ref, table_of_ints, scratch1, scratch2 = refs[18], refs[19], refs[20:24], refs[24:28]
-    load_sem, local_sem, ints_send, ints_recv, hop_send, hop_recv, halo_send, halo_recv = refs[28:36]
-    in_send, in_recv, in_local, back_send, back_recv, out_send, out_recv, out_local = refs[36:]
+def kernel(member_n, space_n, ahead, *refs):
+    sources, states_hbm, tiles_hbm, out_ref, refs = refs[:6], refs[6], refs[7], refs[8], refs[9:]
+    copies, (tiles_ref, table_of_ints, ints_ref), refs = refs[:5], refs[5:8], refs[8:]
+    cell_ref, op_ref, values_ref, weights_ref, table_ref = copies
+    states_ref, cells_ref, picks_ref, win1_ref, win2_ref, acc_ref = refs[:6]
+    scratch1, scratch2, refs = refs[6:10], refs[10:14], refs[14:]
+    load_sem, local_sem, ints_send, ints_recv, hop_send, hop_recv, halo_send, halo_recv = refs[:8]
+    in_send, in_recv, in_local, back_send, back_recv, rest_send, rest_recv = refs[8:15]
+    out_send, out_recv, out_local = refs[15:]
+    codes_hbm = sources[5]
 
     nb, members, _ = cells_ref.shape
-    ob, loc = picks_ref.shape[0], reach_ref.shape[3]
+    ob = picks_ref.shape[0]
     share = states_ref.shape[1]
+    batches = cell_ref.shape[0]
+    loc = codes_hbm.shape[1] // nb
     me = lax.axis_index("member")
     slab = lax.axis_index("space")
     after = lax.rem(slab + 1, space_n)
@@ -111,15 +116,11 @@
     line = member_n // 2
     at, lane = me // 2, lax.rem(me, 2)
     mate = at * 2 + 1 - lane
-
-    def load(block):
-        return pltpu.make_async_copy(
-            columns(states_hbm, block), states_ref.at[block], load_sem.at[block]
-        )
-
-    @pl.loop(0, member_n * nb)
-    def _(block):
-        load(block).start()
+    odd = lax.rem(slab, 2)
+    near, far = 2 * (1 - odd), 2 * odd
+    near_slab = slab + 1 - 2 * odd
+    far_slab = lax.rem(slab + space_n - 1 + 2 * odd, space_n)
+    quarter = members // 4
 
     barrier = pltpu.get_barrier_semaphore()
 
@@ -133,8 +134,31 @@
     for hop_by in range(1, member_n):
         greet(lax.rem(me + hop_by, member_n), slab)
 
+    small = [
+        pltpu.make_async_copy(sources[i], copies[i], local_sem.at[i]) for i in range(len(copies))
+    ]
+    for copy in small:
+        copy.start()
+
+    def load(block):
+        return pltpu.make_async_copy(
+            columns(states_hbm, block), states_ref.at[block], load_sem.at[block]
+        )
+
+    @pl.loop(0, member_n * nb)
+    def _(block):
+        load(block).start()
+
+    tiles_copy = pltpu.make_async_copy(tiles_hbm, tiles_ref, local_sem.at[5])
+    tiles_copy.start()
+    keep_ints = pltpu.make_async_copy(codes_hbm, ints_ref.at[me], local_sem.at[6])
+    keep_ints.start()
+
     def rows(member):
         return pl.ds(pl.multiple_of(member * share, 8), share)
+
+    for copy in small:
+        copy.wait()
 
     @pl.loop(0, member_n * nb)
     def _(block):
@@ -212,29 +236,23 @@
             if hop_by % 2 == 1:
                 take(block, hop_by).start()
 
-    def give_ints(which, hop_by):
+    waiting = list(range(nb))
+
+    def feed(count=1):
+        for _ in range(min(count, len(waiting))):
+            straight(waiting.pop(0))
+
+    def give_ints(hop_by):
         peer = lax.rem(me + hop_by, member_n)
         return send(
-            (reach_src, tile_src)[which].at[0, 0],
-            ints_ref.at[which, me],
-            ints_send.at[which, hop_by],
-            ints_recv.at[which, me],
-            peer,
-            slab,
-        )
-
-    def keep_ints(which):
-        return pltpu.make_async_copy(
-            (reach_src, tile_src)[which].at[0, 0], ints_ref.at[which, me], local_sem.at[1 + which]
+            codes_hbm, ints_ref.at[me], ints_send.at[hop_by], ints_recv.at[me], peer, slab
         )
 
     pass_on(0, me, True, True, True)
-    for which in range(2):
-        for hop_by in range(1, member_n):
-            give_ints(which, hop_by).start()
-        keep_ints(which).start()
+    for hop_by in range(1, member_n):
+        give_ints(hop_by).start()
     pass_on(1, me, True, True, True)
-    straight(0)
+    feed()
 
     for item in range(2):
         for step in range(1, line):
@@ -251,61 +269,51 @@
                 pass_on(item, high, False, True, True)
 
             if step == 1:
-                for b in ([1],[3])[item]:
-                    straight(b)
-            far = 2 * (step - 1)
-            if far == 0:
+                feed()
+            gap = 2 * (step - 1)
+            if gap == 0:
                 landed(item, mate)
                 pass_on(item, mate, False, False, False)
             else:
-                @pl.when(mate - far >= 0)
+                @pl.when(mate - gap >= 0)
                 def _():
-                    landed(item, mate - far)
-                    pass_on(item, mate - far, False, False, False)
-
-                @pl.when(mate + far < member_n)
+                    landed(item, mate - gap)
+                    pass_on(item, mate - gap, False, False, False)
+
+                @pl.when(mate + gap < member_n)
                 def _():
-                    landed(item, mate + far)
-                    pass_on(item, mate + far, False, False, False)
-
-        far = 2 * (line - 1)
-
-        @pl.when(mate - far >= 0)
+                    landed(item, mate + gap)
+                    pass_on(item, mate + gap, False, False, False)
+
+        gap = 2 * (line - 1)
+
+        @pl.when(mate - gap >= 0)
         def _():
-            landed(item, mate - far)
-            pass_on(item, mate - far, False, False, False)
-
-        @pl.when(mate + far < member_n)
+            landed(item, mate - gap)
+            pass_on(item, mate - gap, False, False, False)
+
+        @pl.when(mate + gap < member_n)
         def _():
-            landed(item, mate + far)
-            pass_on(item, mate + far, False, False, False)
+            landed(item, mate + gap)
+            pass_on(item, mate + gap, False, False, False)
 
         if item == 0:
-            pass
-            straight(2)
-
-    for block in range(4, nb):
-        straight(block)
-    for block in range(nb):
+            feed()
+
+    feed(nb)
+
+    @pl.loop(0, nb)
+    def _(block):
         crossing(block)
 
-    for which in range(2):
-        keep_ints(which).wait()
-        for hop_by in range(1, member_n):
-            peer = lax.rem(me + hop_by, member_n)
-            send(
-                (reach_src, tile_src)[which].at[0, 0],
-                ints_ref.at[which, peer],
-                ints_send.at[which, hop_by],
-                ints_recv.at[which, peer],
-                peer,
-                slab,
-            ).wait_recv()
-    scalars = pltpu.make_async_copy(ints_ref, table_of_ints, local_sem.at[3])
+    keep_ints.wait()
+    for hop_by in range(1, member_n):
+        peer = lax.rem(me + hop_by, member_n)
+        send(
+            codes_hbm, ints_ref.at[peer], ints_send.at[hop_by], ints_recv.at[peer], peer, slab
+        ).wait_recv()
+    scalars = pltpu.make_async_copy(ints_ref, table_of_ints, local_sem.at[7])
     scalars.start()
-
-    near = 2 * (1 - lax.rem(slab, 2))
-    far = 2 - near
 
     def source_of(place):
         return lax.rem(slab + space_n - 1 + place, space_n)
@@ -317,33 +325,63 @@
     for place in (near, far):
         load_window(0, place, source_of(place), win1_ref, values_ref, weights_ref, scratch1)
     scalars.wait()
-
-    def back(o, way):
+    tiles_copy.wait()
+
+    def choices(batch, owner, block):
+        return [
+            (
+                table_of_ints[owner, batch, block * loc + l],
+                table_of_ints[owner, batches + batch, block * loc + l],
+            )
+            for l in range(loc)
+        ]
+
+    def back_near(o):
         return send(
             win2_ref.at[1, o],
-            win2_ref.at[2 * way, o],
-            back_send.at[o, way],
-            back_recv.at[o, way],
+            win2_ref.at[far, o],
+            back_send.at[o, 0],
+            back_recv.at[o, 0],
             me,
-            (after, before)[way],
-        )
+            near_slab,
+        )
+
+    def back_far(o):
+        part = pl.ds(pl.multiple_of(lane * quarter, 8), 3 * quarter)
+        return send(
+            win2_ref.at[1, o, part],
+            win2_ref.at[near, o, part],
+            back_send.at[o, 1],
+            back_recv.at[o, 1],
+            me,
+            far_slab,
+        )
+
+    def rest(o, side_of):
+        part = win2_ref.at[far, o, pl.ds(pl.multiple_of(side_of * 3 * quarter, 8), quarter)]
+        return send(part, part, rest_send.at[o], rest_recv.at[o], mate, slab)
+
+    def relay(o):
+        back_far(o).wait_recv()
+        rest(o, lane).start()
 
     @pl.loop(0, ob)
     def _(o):
         cell = cell_ref[1, 0, o]
         owner = cell // nb
-        place = cell - owner * nb
-        picks = [
-            (table_of_ints[0, owner, place, l], table_of_ints[1, owner, place, l])
-            for l in range(loc)
-        ]
+        picks = choices(0, owner, cell - owner * nb)
         fresh = update(picks_ref[o], picks, tiles_ref, scratch1, acc_ref)
         win2_ref[1, o] = observe(fresh, table_ref[op_ref[1, 0, o]])
-        back(o, 0).start()
-        back(o, 1).start()
-
-    @pl.loop(0, nb)
-    def _(block):
+        back_near(o).start()
+        back_far(o).start()
+
+        @pl.when(o >= 2)
+        def _():
+            relay(o - 2)
+
+    load_window(1, 1, slab, win2_ref, values_ref, weights_ref, scratch2)
+
+    def first(block):
         stay(block).wait()
         for hop_by in range(1, member_n):
             peer = lax.rem(me + hop_by, member_n)
@@ -355,15 +393,23 @@
                 peer,
                 slab,
             ).wait_recv()
-        picks = [(reach_ref[0, 0, block, l], tile_ref[0, 0, block, l]) for l in range(loc)]
+        picks = choices(0, me, block)
         cells_ref[block] = update(cells_ref[block], picks, tiles_ref, scratch1, acc_ref)
 
-    load_window(1, 1, slab, win2_ref, values_ref, weights_ref, scratch2)
-    for way in range(2):
-        for o in range(ob):
-            back(o, way).wait_recv()
-    for place in (near, far):
-        load_window(1, place, source_of(place), win2_ref, values_ref, weights_ref, scratch2)
+    @pl.loop(0, ahead)
+    def _(block):
+        first(block)
+
+        @pl.when(block < 2)
+        def _():
+            relay(ob - 2 + block)
+
+    for o in range(ob):
+        back_near(o).wait_recv()
+    load_window(1, near, source_of(near), win2_ref, values_ref, weights_ref, scratch2)
+    for o in range(ob):
+        rest(o, 1 - lane).wait_recv()
+    load_window(1, far, source_of(far), win2_ref, values_ref, weights_ref, scratch2)
 
     def give(block, hop_by):
         peer = lax.rem(me + hop_by, member_n)
@@ -383,15 +429,18 @@
 
     @pl.loop(0, nb)
     def _(block):
-        picks = [(reach_ref[1, 0, block, l], tile_ref[1, 0, block, l]) for l in range(loc)]
+        @pl.when((block >= 2) & (ahead - 2 + block < nb))
+        def _():
+            first(ahead - 2 + block)
+
+        picks = choices(1, me, block)
         cells_ref[block] = update(cells_ref[block], picks, tiles_ref, scratch2, acc_ref)
         for hop_by in hops:
             give(block, hop_by).start()
         keep(block).start()
 
-    for which in range(2):
-        for hop_by in range(1, member_n):
-            give_ints(which, hop_by).wait_send()
+    for hop_by in range(1, member_n):
+        give_ints(hop_by).wait_send()
     for member in range(member_n):
         spot, same = member // 2, lane == member % 2
         for way in range(2):
@@ -409,8 +458,9 @@
             def _():
                 hop(item, member, 2, mate).wait_send()
     for o in range(ob):
-        for way in range(2):
-            back(o, way).wait_send()
+        back_near(o).wait_send()
+        back_far(o).wait_send()
+        rest(o, lane).wait_send()
 
     @pl.loop(0, nb)
     def _(block):
@@ -436,11 +486,10 @@
     share, width = states.shape
     members = share * member_n
     ob = obs_cell.shape[2]
-    nb, loc = loc_obs.shape[2:]
+    batches, _, nb, loc = loc_obs.shape
+    codes = jnp.stack([loc_obs, loc_tile]).reshape(2 * batches, nb * loc)
     f32, bf16, i32 = jnp.float32, jnp.bfloat16, jnp.int32
-    smem = pl.BlockSpec(memory_space=pltpu.SMEM)
-    vmem = pl.BlockSpec(memory_space=pltpu.VMEM)
-    anywhere = pl.BlockSpec(memory_space=pl.ANY)
+    hbm = pl.BlockSpec(memory_space=pltpu.HBM)
     dma = pltpu.SemaphoreType.DMA
     parts = [
         pltpu.VMEM((3 * ob, members, BLK), bf16),
@@ -449,24 +498,30 @@
         pltpu.VMEM((3 * ob, 1, BLK), f32),
     ]
     return pl.pallas_call(
-        functools.partial(kernel, member_n, space_n),
+        functools.partial(kernel, member_n, space_n, max(2, nb - 2)),
         out_shape=jax.ShapeDtypeStruct((share, width), f32),
-        in_specs=[smem] * 4 + [vmem] * 2 + [anywhere] + [vmem] * 4,
-        out_specs=anywhere,
+        in_specs=[hbm] * 8,
+        out_specs=pl.BlockSpec(memory_space=pl.ANY),
         scratch_shapes=[
+            pltpu.SMEM(obs_cell.shape, i32),
+            pltpu.SMEM(op_select.shape, i32),
+            pltpu.VMEM(obs_values.shape, f32),
+            pltpu.VMEM(obs_weights.shape, f32),
+            pltpu.VMEM(op_table.shape, f32),
+            pltpu.VMEM(loc_tiles.shape, f32),
+            pltpu.SMEM((member_n,) + codes.shape, i32),
+            pltpu.VMEM((member_n,) + codes.shape, i32),
             pltpu.VMEM((width // BLK, share, BLK), f32),
             pltpu.VMEM((nb, members, BLK), f32),
             pltpu.VMEM((ob, members, BLK), f32),
             pltpu.VMEM((3, ob, members, BLK), f32),
             pltpu.VMEM((3, ob, members, BLK), f32),
             pltpu.VMEM((members, BLK), f32),
-            pltpu.VMEM((2, member_n, nb, loc), i32),
-            pltpu.SMEM((2, member_n, nb, loc), i32),
         ] + parts + parts + [
             dma((width // BLK,)),
-            dma((4,)),
-            dma((2, member_n)),
-            dma((2, member_n)),
+            dma((8,)),
+            dma((member_n,)),
+            dma((member_n,)),
             dma((2, member_n, 3)),
             dma((2, member_n)),
             dma((member_n, 2)),
@@ -476,6 +531,8 @@
             dma((nb,)),
             dma((ob, 2)),
             dma((ob, 2)),
+            dma((ob,)),
+            dma((ob,)),
             dma((nb, member_n)),
             dma((nb, member_n)),
             dma((nb,)),
@@ -483,10 +540,7 @@
         compiler_params=pltpu.CompilerParams(
             vmem_limit_bytes=58 * 1024 * 1024, collective_id=0, has_side_effects=True
         ),
-    )(
-        obs_cell, op_select, loc_obs, loc_tile, loc_obs, loc_tile,
-        states, obs_values, obs_weights, op_table, loc_tiles,
-    )
+    )(obs_cell, op_select, obs_values, obs_weights, op_table, codes, states, loc_tiles)
 
 
 def solution(mesh):

time: 193 us -> 190 us (0.984)
  Pallas kernels: 187 us -> 183 us
    pallas_call x1, Pallas kernels: 187 us -> 183 us  [per_device(): pl.pallas_call(functools.partial(kernel, member_n, space_n, max(2, nb - 2...]
    unnamed x3 -> x1, local copies, waits for them, and re-layouts: 6.43 us -> 3.86 us
where the time goes in v3:
time: 190 us; the launch traced here: 189 us
  Pallas kernels  183 us (96%)
  local copies, waits for them, and re-layouts  5.23 us (3%)
    pallas_call x1, Pallas kernels, per_device(): pl.pallas_call(functools.partial(kernel, member_n, space_n, max(2, nb - 2...  183 us
    unnamed x1, local copies, waits for them, and re-layouts  3.86 us

profile of v3, /device:TPU:0, one launch (start us, length us, event | category | flops | bytes accessed | tf_op | source)
XLA Modules:
  0.0 188.6 jit_solution(10139997565968305854)
XLA Ops:
  0.0 0.7 copy_bitcast_fusion
  0.7 0.7 reshape.3.refs_5_
  1.4 183.3 %shard_map.91 = f32[128,6144]{1,0:T(8,128)} custom-call(s32[2,1,4]{2,1,0:T(1,128)} %refs_0_.1, s32[2,1,4]{2,1,0:T(1,128)} %refs_1_.1, f32[2,2048]{1,0:T(2,128)} %refs_2_.1, f32[2,2048]{1,0:T(2,128)} %refs_3_.1, f32[8,128,128]{2,1,0:T(8,128)} %refs_4_.1, s32[4,48]{1,0:T(4,128)} %reshape.3.refs_5_, f32[128,6144]{1,0:T(8,128)} %refs_6_.1, f32[8,128,128]{2,1,0:T(8,128)} %refs_7_.1), custom_call_target="tpu_custom_call" | custom-call | tf_op jit(solution)/shard_map/pallas_call | solution.py:500
  184.7 3.9 %copy.19 = f32[128,6144]{1,0:T(8,128)} copy(f32[128,6144]{1,0:T(8,128)} %shard_map.91) | data formatting | bytes 6291456
  (2 shorter events, 0.0 us)

commit v4 on v3

--- a/solution.py
+++ b/solution.py
@@ -47,23 +47,27 @@
     return ref.at[:, pl.ds(pl.multiple_of(block * BLK, BLK), BLK)]
 
 
-def load_window(batch, place, source, window_ref, values_ref, weights_ref, scratch):
-    hi_ref, lo_ref, d_ref, w_ref = scratch[:4]
+def load_block(batch, place, o, source, window_ref, values_ref, weights_ref, scratch):
+    hi_ref, lo_ref, d_ref, w_ref = scratch
     _, ob, members, _ = window_ref.shape
-    for o in range(ob):
-        j = place * ob + o
-        at = pl.ds(pl.multiple_of((source * ob + o) * BLK, BLK), BLK)
-        weight = weights_ref[batch:batch + 1, at]
-        block = window_ref[place, o]
-        mean = jnp.sum(block, axis=0, keepdims=True) * (1.0 / members)
-        hi, lo = split(block - mean)
-        hi_ref[j] = hi
-        lo_ref[j] = lo
-        w_ref[j] = weight
-        d_ref[j] = weight * (values_ref[batch:batch + 1, at] - mean)
-
-
-def update(cell, picks, tiles_ref, scratch, acc_ref):
+    j = place * ob + o
+    at = pl.ds(pl.multiple_of((source * ob + o) * BLK, BLK), BLK)
+    weight = weights_ref[batch:batch + 1, at]
+    block = window_ref[place, o]
+    mean = jnp.sum(block, axis=0, keepdims=True) * (1.0 / members)
+    hi, lo = split(block - mean)
+    hi_ref[j] = hi
+    lo_ref[j] = lo
+    w_ref[j] = weight
+    d_ref[j] = weight * (values_ref[batch:batch + 1, at] - mean)
+
+
+def load_window(batch, place, source, window_ref, *rest):
+    for o in range(window_ref.shape[1]):
+        load_block(batch, place, o, source, window_ref, *rest)
+
+
+def gains(cell, picks, tiles_ref, scratch, gain_ref):
     hi_ref, lo_ref, d_ref, w_ref = scratch
     members = cell.shape[0]
     mean = jnp.sum(cell, axis=0, keepdims=True) * (1.0 / members)
@@ -82,26 +86,29 @@
         w = jnp.concatenate([w_ref[first], w_ref[second]], axis=1)
         ones.append(jnp.sum(gain * d, axis=1, keepdims=True))
         gain_hi, gain_lo = split(gain * (-0.5 * w))
-        step = dot_nt(obs_hi, jnp.concatenate([gain_hi, gain_lo], axis=0))
-        step = step[:, :BLK] + step[:, BLK:] + dot_nt(obs_lo, gain_hi)
-        if pair == 0:
-            acc_ref[...] = step
-        else:
-            acc_ref[...] += step
+        gain_ref[:BLK, 2 * pair * BLK:2 * (pair + 1) * BLK] = gain_hi
+        gain_ref[BLK:, 2 * pair * BLK:2 * (pair + 1) * BLK] = gain_lo
     shift = functools.reduce(jnp.add, ones)
-    row = jnp.transpose(jnp.broadcast_to(shift, (BLK, BLK)))[:1]
-    return cell + (acc_ref[...] + row)
+    return jnp.transpose(jnp.broadcast_to(shift, (BLK, BLK)))[:1]
+
+
+def moved(part, at, picks, row, scratch, gain_ref):
+    hi_ref, lo_ref = scratch[:2]
+    obs_hi = jnp.concatenate([hi_ref[j, at] for j, _ in picks], axis=1)
+    obs_lo = jnp.concatenate([lo_ref[j, at] for j, _ in picks], axis=1)
+    step = dot_nt(obs_hi, gain_ref[...])
+    return part + (step[:, :BLK] + step[:, BLK:] + dot_nt(obs_lo, gain_ref[:BLK]) + row)
 
 
 def kernel(member_n, space_n, ahead, *refs):
     sources, states_hbm, tiles_hbm, out_ref, refs = refs[:6], refs[6], refs[7], refs[8], refs[9:]
     copies, (tiles_ref, table_of_ints, ints_ref), refs = refs[:5], refs[5:8], refs[8:]
     cell_ref, op_ref, values_ref, weights_ref, table_ref = copies
-    states_ref, cells_ref, picks_ref, win1_ref, win2_ref, acc_ref = refs[:6]
+    states_ref, cells_ref, picks_ref, win1_ref, win2_ref, gain_ref = refs[:6]
     scratch1, scratch2, refs = refs[6:10], refs[10:14], refs[14:]
     load_sem, local_sem, ints_send, ints_recv, hop_send, hop_recv, halo_send, halo_recv = refs[:8]
     in_send, in_recv, in_local, back_send, back_recv, rest_send, rest_recv = refs[8:15]
-    out_send, out_recv, out_local = refs[15:]
+    far_send, far_recv, out_send, out_recv, out_local = refs[15:]
     codes_hbm = sources[5]
 
     nb, members, _ = cells_ref.shape
@@ -340,29 +347,31 @@
         return send(
             win2_ref.at[1, o],
             win2_ref.at[far, o],
-            back_send.at[o, 0],
-            back_recv.at[o, 0],
+            back_send.at[o],
+            back_recv.at[o],
             me,
             near_slab,
         )
 
-    def back_far(o):
-        part = pl.ds(pl.multiple_of(lane * quarter, 8), 3 * quarter)
+    def rows_of(q):
+        return pl.ds(pl.multiple_of(q * quarter, 16), quarter)
+
+    def back_far(o, q):
         return send(
-            win2_ref.at[1, o, part],
-            win2_ref.at[near, o, part],
-            back_send.at[o, 1],
-            back_recv.at[o, 1],
+            win2_ref.at[1, o, rows_of(q)],
+            win2_ref.at[near, o, rows_of(q)],
+            far_send.at[o, q],
+            far_recv.at[o, q],
             me,
             far_slab,
         )
 
     def rest(o, side_of):
-        part = win2_ref.at[far, o, pl.ds(pl.multiple_of(side_of * 3 * quarter, 8), quarter)]
+        part = win2_ref.at[far, o, rows_of(side_of * 3)]
         return send(part, part, rest_send.at[o], rest_recv.at[o], mate, slab)
 
     def relay(o):
-        back_far(o).wait_recv()
+        back_far(o, lane * 3).wait_recv()
         rest(o, lane).start()
 
     @pl.loop(0, ob)
@@ -370,10 +379,21 @@
         cell = cell_ref[1, 0, o]
         owner = cell // nb
         picks = choices(0, owner, cell - owner * nb)
-        fresh = update(picks_ref[o], picks, tiles_ref, scratch1, acc_ref)
-        win2_ref[1, o] = observe(fresh, table_ref[op_ref[1, 0, o]])
+        row = gains(picks_ref[o], picks, tiles_ref, scratch1, gain_ref)
+        operator = table_ref[op_ref[1, 0, o]]
+
+        @pl.loop(0, 4)
+        def _(turn):
+            q = turn + lane * (3 - 2 * turn)
+            at_q = rows_of(q)
+            fresh = moved(picks_ref[o, at_q], at_q, picks, row, scratch1, gain_ref)
+            win2_ref[1, o, at_q] = observe(fresh, operator)
+
+            @pl.when(turn < 3)
+            def _():
+                back_far(o, q).start()
+
         back_near(o).start()
-        back_far(o).start()
 
         @pl.when(o >= 2)
         def _():
@@ -394,7 +414,13 @@
                 slab,
             ).wait_recv()
         picks = choices(0, me, block)
-        cells_ref[block] = update(cells_ref[block], picks, tiles_ref, scratch1, acc_ref)
+        row = gains(cells_ref[block], picks, tiles_ref, scratch1, gain_ref)
+
+        @pl.loop(0, 4)
+        def _(q):
+            at_q = rows_of(q)
+            part = cells_ref[block, at_q]
+            cells_ref[block, at_q] = moved(part, at_q, picks, row, scratch1, gain_ref)
 
     @pl.loop(0, ahead)
     def _(block):
@@ -408,15 +434,16 @@
         back_near(o).wait_recv()
     load_window(1, near, source_of(near), win2_ref, values_ref, weights_ref, scratch2)
     for o in range(ob):
+        back_far(o, 1).wait_recv()
+        back_far(o, 2).wait_recv()
         rest(o, 1 - lane).wait_recv()
-    load_window(1, far, source_of(far), win2_ref, values_ref, weights_ref, scratch2)
-
-    def give(block, hop_by):
-        peer = lax.rem(me + hop_by, member_n)
+        load_block(1, far, o, source_of(far), win2_ref, values_ref, weights_ref, scratch2)
+
+    def give(block, peer):
         return send(
             cells_ref.at[block, rows(peer)],
             columns(out_ref, me * nb + block),
-            out_send.at[block, hop_by],
+            out_send.at[block, peer],
             out_recv.at[block, me],
             peer,
             slab,
@@ -426,6 +453,9 @@
         return pltpu.make_async_copy(
             cells_ref.at[block, rows(me)], columns(out_ref, me * nb + block), out_local.at[block]
         )
+
+    opposite = jnp.where(at < line // 2, 2, 0)
+    group = member_n // 4
 
     @pl.loop(0, nb)
     def _(block):
@@ -434,10 +464,24 @@
             first(ahead - 2 + block)
 
         picks = choices(1, me, block)
-        cells_ref[block] = update(cells_ref[block], picks, tiles_ref, scratch2, acc_ref)
-        for hop_by in hops:
-            give(block, hop_by).start()
-        keep(block).start()
+        row = gains(cells_ref[block], picks, tiles_ref, scratch2, gain_ref)
+
+        @pl.loop(0, 4)
+        def _(turn):
+            q = lax.rem(turn + opposite, 4)
+            at_q = rows_of(q)
+            part = cells_ref[block, at_q]
+            cells_ref[block, at_q] = moved(part, at_q, picks, row, scratch2, gain_ref)
+            for k in range(group):
+                peer = q * group + k
+
+                @pl.when(peer != me)
+                def _():
+                    give(block, peer).start()
+
+                @pl.when(peer == me)
+                def _():
+                    keep(block).start()
 
     for hop_by in range(1, member_n):
         give_ints(hop_by).wait_send()
@@ -459,7 +503,8 @@
                 hop(item, member, 2, mate).wait_send()
     for o in range(ob):
         back_near(o).wait_send()
-        back_far(o).wait_send()
+        for turn in range(3):
+            back_far(o, turn + lane * (3 - 2 * turn)).wait_send()
         rest(o, lane).wait_send()
 
     @pl.loop(0, nb)
@@ -467,12 +512,12 @@
         keep(block).wait()
         for hop_by in range(1, member_n):
             take(block, hop_by).wait_send()
-            give(block, hop_by).wait_send()
             peer = lax.rem(me + hop_by, member_n)
+            give(block, peer).wait_send()
             send(
                 cells_ref.at[block, rows(peer)],
                 columns(out_ref, peer * nb + block),
-                out_send.at[block, hop_by],
+                out_send.at[block, peer],
                 out_recv.at[block, peer],
                 peer,
                 slab,
@@ -498,7 +543,7 @@
         pltpu.VMEM((3 * ob, 1, BLK), f32),
     ]
     return pl.pallas_call(
-        functools.partial(kernel, member_n, space_n, max(2, nb - 2)),
+        functools.partial(kernel, member_n, space_n, max(2, nb - 3)),
         out_shape=jax.ShapeDtypeStruct((share, width), f32),
         in_specs=[hbm] * 8,
         out_specs=pl.BlockSpec(memory_space=pl.ANY),
@@ -516,7 +561,7 @@
             pltpu.VMEM((ob, members, BLK), f32),
             pltpu.VMEM((3, ob, members, BLK), f32),
             pltpu.VMEM((3, ob, members, BLK), f32),
-            pltpu.VMEM((members, BLK), f32),
+            pltpu.VMEM((2 * BLK, loc * BLK), bf16),
         ] + parts + parts + [
             dma((width // BLK,)),
             dma((8,)),
@@ -529,10 +574,12 @@
             dma((nb, member_n)),
             dma((nb, member_n)),
             dma((nb,)),
-            dma((ob, 2)),
-            dma((ob, 2)),
             dma((ob,)),
             dma((ob,)),
+            dma((ob,)),
+            dma((ob,)),
+            dma((ob, 4)),
+            dma((ob, 4)),
             dma((nb, member_n)),
             dma((nb, member_n)),
             dma((nb,)),

time: 190 us -> 187 us (0.984)
  Pallas kernels: 183 us -> 181 us
    pallas_call x1, Pallas kernels: 183 us -> 181 us  [per_device(): pl.pallas_call(functools.partial(kernel, member_n, space_n, max(2, nb - 3...]
where the time goes in v4:
time: 187 us; the launch traced here: 186 us
  Pallas kernels  181 us (97%)
  local copies, waits for them, and re-layouts  5.23 us (3%)
    pallas_call x1, Pallas kernels, per_device(): pl.pallas_call(functools.partial(kernel, member_n, space_n, max(2, nb - 3...  181 us
    unnamed x1, local copies, waits for them, and re-layouts  3.86 us

profile of v4, /device:TPU:0, one launch (start us, length us, event | category | flops | bytes accessed | tf_op | source)
XLA Modules:
  0.0 186.4 jit_solution(17834232521531898302)
XLA Ops:
  0.0 0.7 copy_bitcast_fusion
  0.7 0.7 reshape.3.refs_5_
  1.4 181.1 %shard_map.91 = f32[128,6144]{1,0:T(8,128)} custom-call(s32[2,1,4]{2,1,0:T(1,128)} %refs_0_.1, s32[2,1,4]{2,1,0:T(1,128)} %refs_1_.1, f32[2,2048]{1,0:T(2,128)} %refs_2_.1, f32[2,2048]{1,0:T(2,128)} %refs_3_.1, f32[8,128,128]{2,1,0:T(8,128)} %refs_4_.1, s32[4,48]{1,0:T(4,128)} %reshape.3.refs_5_, f32[128,6144]{1,0:T(8,128)} %refs_6_.1, f32[8,128,128]{2,1,0:T(8,128)} %refs_7_.1), custom_call_target="tpu_custom_call" | custom-call | tf_op jit(solution)/shard_map/pallas_call | solution.py:545
  182.5 3.9 %copy.19 = f32[128,6144]{1,0:T(8,128)} copy(f32[128,6144]{1,0:T(8,128)} %shard_map.91) | data formatting | bytes 6291456
  (2 shorter events, 0.0 us)

commit v5 on v4

--- a/solution.py
+++ b/solution.py
@@ -111,7 +111,8 @@
     far_send, far_recv, out_send, out_recv, out_local = refs[15:]
     codes_hbm = sources[5]
 
-    nb, members, _ = cells_ref.shape
+    slots, members, _ = cells_ref.shape
+    nb = slots - 1
     ob = picks_ref.shape[0]
     share = states_ref.shape[1]
     batches = cell_ref.shape[0]
@@ -128,6 +129,15 @@
     near_slab = slab + 1 - 2 * odd
     far_slab = lax.rem(slab + space_n - 1 + 2 * odd, space_n)
     quarter = members // 4
+    half = member_n // 2
+    partner = lax.rem(me + half, member_n)
+
+    def block_of(member, slot):
+        other = lax.rem(member + half, member_n)
+        return jnp.where(slot < nb, member * nb + slot, other * nb + nb - 1)
+
+    def reached(member, slot):
+        return (slot < nb - 1) | (member // half == me // half)
 
     barrier = pltpu.get_barrier_semaphore()
 
@@ -217,7 +227,7 @@
     def take(block, hop_by):
         peer = lax.rem(me + hop_by, member_n)
         return send(
-            states_ref.at[peer * nb + block],
+            states_ref.at[block_of(peer, block)],
             cells_ref.at[block, rows(me)],
             in_send.at[block, hop_by],
             in_recv.at[block, me],
@@ -227,7 +237,7 @@
 
     def stay(block):
         return pltpu.make_async_copy(
-            states_ref.at[me * nb + block], cells_ref.at[block, rows(me)], in_local.at[block]
+            states_ref.at[block_of(me, block)], cells_ref.at[block, rows(me)], in_local.at[block]
         )
 
     hops = sorted(range(1, member_n), key=lambda k: (abs(k - line), k))
@@ -243,7 +253,7 @@
             if hop_by % 2 == 1:
                 take(block, hop_by).start()
 
-    waiting = list(range(nb))
+    waiting = list(range(slots))
 
     def feed(count=1):
         for _ in range(min(count, len(waiting))):
@@ -307,9 +317,9 @@
         if item == 0:
             feed()
 
-    feed(nb)
-
-    @pl.loop(0, nb)
+    feed(slots)
+
+    @pl.loop(0, slots)
     def _(block):
         crossing(block)
 
@@ -334,6 +344,10 @@
     scalars.wait()
     tiles_copy.wait()
 
+    def choices_of(batch, slot):
+        owner = jnp.where(slot < nb, me, partner)
+        return choices(batch, owner, jnp.where(slot < nb, slot, nb - 1))
+
     def choices(batch, owner, block):
         return [
             (
@@ -389,15 +403,10 @@
             fresh = moved(picks_ref[o, at_q], at_q, picks, row, scratch1, gain_ref)
             win2_ref[1, o, at_q] = observe(fresh, operator)
 
-            @pl.when(turn < 3)
-            def _():
-                back_far(o, q).start()
+            back_far(o, q).start()
 
         back_near(o).start()
 
-        @pl.when(o >= 2)
-        def _():
-            relay(o - 2)
 
     load_window(1, 1, slab, win2_ref, values_ref, weights_ref, scratch2)
 
@@ -406,14 +415,14 @@
         for hop_by in range(1, member_n):
             peer = lax.rem(me + hop_by, member_n)
             send(
-                states_ref.at[peer * nb + block],
+                states_ref.at[block_of(peer, block)],
                 cells_ref.at[block, rows(peer)],
                 in_send.at[block, hop_by],
                 in_recv.at[block, peer],
                 peer,
                 slab,
             ).wait_recv()
-        picks = choices(0, me, block)
+        picks = choices_of(0, block)
         row = gains(cells_ref[block], picks, tiles_ref, scratch1, gain_ref)
 
         @pl.loop(0, 4)
@@ -426,23 +435,19 @@
     def _(block):
         first(block)
 
-        @pl.when(block < 2)
-        def _():
-            relay(ob - 2 + block)
 
     for o in range(ob):
         back_near(o).wait_recv()
     load_window(1, near, source_of(near), win2_ref, values_ref, weights_ref, scratch2)
     for o in range(ob):
-        back_far(o, 1).wait_recv()
-        back_far(o, 2).wait_recv()
-        rest(o, 1 - lane).wait_recv()
+        for q in range(4):
+            back_far(o, q).wait_recv()
         load_block(1, far, o, source_of(far), win2_ref, values_ref, weights_ref, scratch2)
 
     def give(block, peer):
         return send(
             cells_ref.at[block, rows(peer)],
-            columns(out_ref, me * nb + block),
+            columns(out_ref, block_of(me, block)),
             out_send.at[block, peer],
             out_recv.at[block, me],
             peer,
@@ -451,23 +456,22 @@
 
     def keep(block):
         return pltpu.make_async_copy(
-            cells_ref.at[block, rows(me)], columns(out_ref, me * nb + block), out_local.at[block]
+            cells_ref.at[block, rows(me)], columns(out_ref, block_of(me, block)), out_local.at[block]
         )
 
     opposite = jnp.where(at < line // 2, 2, 0)
     group = member_n // 4
 
-    @pl.loop(0, nb)
+    @pl.loop(0, slots)
     def _(block):
-        @pl.when((block >= 2) & (ahead - 2 + block < nb))
+        @pl.when((block >= 2) & (ahead - 2 + block < slots))
         def _():
             first(ahead - 2 + block)
 
-        picks = choices(1, me, block)
+        picks = choices_of(1, block)
         row = gains(cells_ref[block], picks, tiles_ref, scratch2, gain_ref)
 
-        @pl.loop(0, 4)
-        def _(turn):
+        def part_of(turn):
             q = lax.rem(turn + opposite, 4)
             at_q = rows_of(q)
             part = cells_ref[block, at_q]
@@ -482,6 +486,12 @@
                 @pl.when(peer == me)
                 def _():
                     keep(block).start()
+
+        @pl.loop(0, 4)
+        def _(turn):
+            @pl.when((turn >= 2) | (block < nb - 1))
+            def _():
+                part_of(turn)
 
     for hop_by in range(1, member_n):
         give_ints(hop_by).wait_send()
@@ -503,25 +513,27 @@
                 hop(item, member, 2, mate).wait_send()
     for o in range(ob):
         back_near(o).wait_send()
-        for turn in range(3):
-            back_far(o, turn + lane * (3 - 2 * turn)).wait_send()
-        rest(o, lane).wait_send()
-
-    @pl.loop(0, nb)
+        for q in range(4):
+            back_far(o, q).wait_send()
+
+    @pl.loop(0, slots)
     def _(block):
         keep(block).wait()
         for hop_by in range(1, member_n):
             take(block, hop_by).wait_send()
             peer = lax.rem(me + hop_by, member_n)
-            give(block, peer).wait_send()
-            send(
-                cells_ref.at[block, rows(peer)],
-                columns(out_ref, peer * nb + block),
-                out_send.at[block, peer],
-                out_recv.at[block, peer],
-                peer,
-                slab,
-            ).wait_recv()
+
+            @pl.when(reached(peer, block))
+            def _():
+                give(block, peer).wait_send()
+                send(
+                    cells_ref.at[block, rows(peer)],
+                    columns(out_ref, block_of(peer, block)),
+                    out_send.at[block, peer],
+                    out_recv.at[block, peer],
+                    peer,
+                    slab,
+                ).wait_recv()
 
 
 def per_device(
@@ -557,7 +569,7 @@
             pltpu.SMEM((member_n,) + codes.shape, i32),
             pltpu.VMEM((member_n,) + codes.shape, i32),
             pltpu.VMEM((width // BLK, share, BLK), f32),
-            pltpu.VMEM((nb, members, BLK), f32),
+            pltpu.VMEM((nb + 1, members, BLK), f32),
             pltpu.VMEM((ob, members, BLK), f32),
             pltpu.VMEM((3, ob, members, BLK), f32),
             pltpu.VMEM((3, ob, members, BLK), f32),
@@ -571,18 +583,18 @@
             dma((2, member_n)),
             dma((member_n, 2)),
             dma((member_n, 2)),
-            dma((nb, member_n)),
-            dma((nb, member_n)),
-            dma((nb,)),
+            dma((nb + 1, member_n)),
+            dma((nb + 1, member_n)),
+            dma((nb + 1,)),
             dma((ob,)),
             dma((ob,)),
             dma((ob,)),
             dma((ob,)),
             dma((ob, 4)),
             dma((ob, 4)),
-            dma((nb, member_n)),
-            dma((nb, member_n)),
-            dma((nb,)),
+            dma((nb + 1, member_n)),
+            dma((nb + 1, member_n)),
+            dma((nb + 1,)),
         ],
         compiler_params=pltpu.CompilerParams(
             vmem_limit_bytes=58 * 1024 * 1024, collective_id=0, has_side_effects=True

time: 187 us -> 185 us (0.989)
  Pallas kernels: 181 us -> 178 us
    pallas_call x1, Pallas kernels: 181 us -> 178 us  [per_device(): pl.pallas_call(functools.partial(kernel, member_n, space_n, max(2, nb - 3...]
where the time goes in v5:
time: 185 us; the launch traced here: 183 us
  Pallas kernels  178 us (96%)
  local copies, waits for them, and re-layouts  5.23 us (3%)
    pallas_call x1, Pallas kernels, per_device(): pl.pallas_call(functools.partial(kernel, member_n, space_n, max(2, nb - 3...  178 us
    unnamed x1, local copies, waits for them, and re-layouts  3.86 us

profile of v5, /device:TPU:0, one launch (start us, length us, event | category | flops | bytes accessed | tf_op | source)
XLA Modules:
  0.0 183.3 jit_solution(9036689556736215033)
XLA Ops:
  0.0 0.7 copy_bitcast_fusion
  0.7 0.7 reshape.3.refs_5_
  1.4 178.1 %shard_map.91 = f32[128,6144]{1,0:T(8,128)} custom-call(s32[2,1,4]{2,1,0:T(1,128)} %refs_0_.1, s32[2,1,4]{2,1,0:T(1,128)} %refs_1_.1, f32[2,2048]{1,0:T(2,128)} %refs_2_.1, f32[2,2048]{1,0:T(2,128)} %refs_3_.1, f32[8,128,128]{2,1,0:T(8,128)} %refs_4_.1, s32[4,48]{1,0:T(4,128)} %reshape.3.refs_5_, f32[128,6144]{1,0:T(8,128)} %refs_6_.1, f32[8,128,128]{2,1,0:T(8,128)} %refs_7_.1), custom_call_target="tpu_custom_call" | custom-call | tf_op jit(solution)/shard_map/pallas_call | solution.py:557
  179.5 3.9 %copy.19 = f32[128,6144]{1,0:T(8,128)} copy(f32[128,6144]{1,0:T(8,128)} %shard_map.91) | data formatting | bytes 6291456
  (2 shorter events, 0.0 us)

commit v6 on v5

--- a/solution.py
+++ b/solution.py
@@ -107,8 +107,8 @@
     states_ref, cells_ref, picks_ref, win1_ref, win2_ref, gain_ref = refs[:6]
     scratch1, scratch2, refs = refs[6:10], refs[10:14], refs[14:]
     load_sem, local_sem, ints_send, ints_recv, hop_send, hop_recv, halo_send, halo_recv = refs[:8]
-    in_send, in_recv, in_local, back_send, back_recv, rest_send, rest_recv = refs[8:15]
-    far_send, far_recv, out_send, out_recv, out_local = refs[15:]
+    in_send, in_recv, in_local, back_send, back_recv = refs[8:13]
+    far_send, far_recv, out_send, out_recv, out_local = refs[13:]
     codes_hbm = sources[5]
 
     slots, members, _ = cells_ref.shape
@@ -380,14 +380,6 @@
             far_slab,
         )
 
-    def rest(o, side_of):
-        part = win2_ref.at[far, o, rows_of(side_of * 3)]
-        return send(part, part, rest_send.at[o], rest_recv.at[o], mate, slab)
-
-    def relay(o):
-        back_far(o, lane * 3).wait_recv()
-        rest(o, lane).start()
-
     @pl.loop(0, ob)
     def _(o):
         cell = cell_ref[1, 0, o]
@@ -398,7 +390,7 @@
 
         @pl.loop(0, 4)
         def _(turn):
-            q = turn + lane * (3 - 2 * turn)
+            q = turn
             at_q = rows_of(q)
             fresh = moved(picks_ref[o, at_q], at_q, picks, row, scratch1, gain_ref)
             win2_ref[1, o, at_q] = observe(fresh, operator)
@@ -534,6 +526,42 @@
                     peer,
                     slab,
                 ).wait_recv()
+
+
+def copy_kernel(source_ref, out_ref, buffer_ref, load_sem, store_sem):
+    steps, tall = load_sem.shape[0], source_ref.shape[0] // load_sem.shape[0]
+
+    def load(i):
+        at = pl.ds(i * tall, tall)
+        return pltpu.make_async_copy(source_ref.at[at], buffer_ref.at[at], load_sem.at[i])
+
+    def store(i):
+        at = pl.ds(i * tall, tall)
+        return pltpu.make_async_copy(buffer_ref.at[at], out_ref.at[at], store_sem.at[i])
+
+    for i in range(steps):
+        load(i).start()
+    for i in range(steps):
+        load(i).wait()
+        store(i).start()
+    for i in range(steps):
+        store(i).wait()
+
+
+def copied(array):
+    steps = max(1, array.shape[0] // 8)
+    return pl.pallas_call(
+        copy_kernel,
+        out_shape=jax.ShapeDtypeStruct(array.shape, array.dtype),
+        in_specs=[pl.BlockSpec(memory_space=pl.ANY)],
+        out_specs=pl.BlockSpec(memory_space=pl.ANY),
+        scratch_shapes=[
+            pltpu.VMEM(array.shape, array.dtype),
+            pltpu.SemaphoreType.DMA((steps,)),
+            pltpu.SemaphoreType.DMA((steps,)),
+        ],
+        compiler_params=pltpu.CompilerParams(vmem_limit_bytes=58 * 1024 * 1024),
+    )(array)
 
 
 def per_device(
@@ -554,8 +582,8 @@
         pltpu.VMEM((3 * ob, 1, BLK), f32),
         pltpu.VMEM((3 * ob, 1, BLK), f32),
     ]
-    return pl.pallas_call(
-        functools.partial(kernel, member_n, space_n, max(2, nb - 3)),
+    result = pl.pallas_call(
+        functools.partial(kernel, member_n, space_n, 2),
         out_shape=jax.ShapeDtypeStruct((share, width), f32),
         in_specs=[hbm] * 8,
         out_specs=pl.BlockSpec(memory_space=pl.ANY),
@@ -588,8 +616,6 @@
             dma((nb + 1,)),
             dma((ob,)),
             dma((ob,)),
-            dma((ob,)),
-            dma((ob,)),
             dma((ob, 4)),
             dma((ob, 4)),
             dma((nb + 1, member_n)),
@@ -600,6 +626,7 @@
             vmem_limit_bytes=58 * 1024 * 1024, collective_id=0, has_side_effects=True
         ),
     )(obs_cell, op_select, obs_values, obs_weights, op_table, codes, states, loc_tiles)
+    return copied(result)
 
 
 def solution(mesh):

time: 185 us -> 181 us (0.978)
  local copies, waits for them, and re-layouts: 5.23 us -> 1.38 us
    unnamed x1 -> x0, local copies, waits for them, and re-layouts: 3.86 us -> none
    pallas_call x1 -> x2, Pallas kernels: 178 us -> 177 us  [the longest x1 174 us: per_device(): pl.pallas_call(functools.partial(kernel, member_n, space_n, 2), out_shape...]
where the time goes in v6:
time: 181 us; the launch traced here: 179 us
  Pallas kernels  177 us (98%)
    pallas_call x1, Pallas kernels, per_device(): pl.pallas_call(functools.partial(kernel, member_n, space_n, 2), out_shape...  174 us

profile of v6, /device:TPU:0, one launch (start us, length us, event | category | flops | bytes accessed | tf_op | source)
XLA Modules:
  0.0 178.8 jit_solution(10752158024414831792)
XLA Ops:
  0.0 0.7 copy_bitcast_fusion
  0.7 0.7 reshape.3.refs_5_
  1.4 174.2 %shard_map.91.source_ref = f32[128,6144]{1,0:T(8,128)} custom-call(s32[2,1,4]{2,1,0:T(1,128)} %refs_0_.1, s32[2,1,4]{2,1,0:T(1,128)} %refs_1_.1, f32[2,2048]{1,0:T(2,128)} %refs_2_.1, f32[2,2048]{1,0:T(2,128)} %refs_3_.1, f32[8,128,128]{2,1,0:T(8,128)} %refs_4_.1, s32[4,48]{1,0:T(4,128)} %reshape.3.refs_5_, f32[128,6144]{1,0:T(8,128)} %refs_6_.1, ...), custom_call_target="tpu_custom_call" | custom-call | tf_op jit(solution)/shard_map/pallas_call | solution.py:585
  175.6 3.2 %shard_map.92 = f32[128,6144]{1,0:T(8,128)} custom-call(f32[128,6144]{1,0:T(8,128)} %shard_map.91.source_ref), custom_call_target="tpu_custom_call" | custom-call | tf_op jit(solution)/shard_map/pallas_call | solution.py:553
  (2 shorter events, 0.0 us)

commit v7 on v6

--- a/solution.py
+++ b/solution.py
@@ -285,7 +285,7 @@
                 landed(item, high)
                 pass_on(item, high, False, True, True)
 
-            if step == 1:
+            if item == 1:
                 feed()
             gap = 2 * (step - 1)
             if gap == 0:

time: 181 us -> 179 us (0.989); the launches traced: 179 us -> 179 us
  no operation moved by 1% of the time
where the time goes in v7:
time: 179 us
  Pallas kernels  178 us (99%)
    pallas_call x1, Pallas kernels, per_device(): pl.pallas_call(functools.partial(kernel, member_n, space_n, 2), out_shape...  174 us

profile of v7, /device:TPU:0, one launch (start us, length us, event | category | flops | bytes accessed | tf_op | source)
XLA Modules:
  0.0 179.0 jit_solution(15807190295613734529)
XLA Ops:
  0.0 0.7 copy_bitcast_fusion
  0.7 0.7 reshape.3.refs_5_
  1.4 174.5 %shard_map.91.source_ref = f32[128,6144]{1,0:T(8,128)} custom-call(s32[2,1,4]{2,1,0:T(1,128)} %refs_0_.1, s32[2,1,4]{2,1,0:T(1,128)} %refs_1_.1, f32[2,2048]{1,0:T(2,128)} %refs_2_.1, f32[2,2048]{1,0:T(2,128)} %refs_3_.1, f32[8,128,128]{2,1,0:T(8,128)} %refs_4_.1, s32[4,48]{1,0:T(4,128)} %reshape.3.refs_5_, f32[128,6144]{1,0:T(8,128)} %refs_6_.1, ...), custom_call_target="tpu_custom_call" | custom-call | tf_op jit(solution)/shard_map/pallas_call | solution.py:585
  175.9 3.2 %shard_map.92 = f32[128,6144]{1,0:T(8,128)} custom-call(f32[128,6144]{1,0:T(8,128)} %shard_map.91.source_ref), custom_call_target="tpu_custom_call" | custom-call | tf_op jit(solution)/shard_map/pallas_call | solution.py:553
  (2 shorter events, 0.0 us)
